TPU v7x, 32 devices: a whole 2x2x4 slice. The times are simulated.
32 devices in a mesh: dp: 2 (over y), tm: 8 (over z, x), height: 2 (over core).
Axes of the slice: x: 2, y: 2, z: 4, core: 2. Of those that a mesh axis runs over, the one named last changes fastest.
Arguments:
- queries: bfloat16 [2, 16, 16, 8, 1536], P('dp', 'tm', 'height'), may hold values from -6 to 6
- keys: bfloat16 [2, 16, 16, 8, 1536], P('dp', 'tm', 'height'), may hold values from -6 to 6
- values: bfloat16 [2, 16, 16, 8, 1536], P('dp', 'tm', 'height'), may hold values from -6 to 6
- text_keys: bfloat16 [2, 256, 1536], P('dp'), may hold values from -110 to 110
- text_values: bfloat16 [2, 256, 1536], P('dp'), may hold values from -6 to 6
- gain_q: float32 [128], replicated, may hold values from 0.5 to 1.5
- gain_k: float32 [128], replicated, may hold values from 0.5 to 1.5
- window_ext: int32 [12, 3], replicated, may hold values from 0 to 1, as said below
- text_len: int32 [2], P('dp'), may hold values from 64 to 256, as said below
- out_grad: bfloat16 [2, 16, 16, 8, 1536], P('dp', 'tm', 'height'), may hold values from -60 to 60
Outputs:
- query_grad: bfloat16 [2, 16, 16, 8, 1536], P('dp', 'tm', 'height')
- key_grad: bfloat16 [2, 16, 16, 8, 1536], P('dp', 'tm', 'height')
- value_grad: bfloat16 [2, 16, 16, 8, 1536], P('dp', 'tm', 'height')
- text_key_grad: float32 [2, 256, 1536], P('dp')
- text_value_grad: float32 [2, 256, 1536], P('dp')
- gain_grads: float32 [2, 128], replicated
Inputs may be any that keep to these rules, and one draw needn't show every extreme that they name: `window_ext`: along each of the three axes some head has reach 1. `text_len`: some sample has all 256 text tokens live.
All inputs are finite; a program needn't handle non-finite values.
Results may differ from a plain program's by a relative error of at most 0.0055.
The roundings to bfloat16 on the way count: a program that leaves them out, or rounds other values in their place, can miss the bound.
Values may be sent and summed in bfloat16 or wider, within the bound.
No kernel may reach another device: no remote copies, remote signals or barrier semaphores. Data moves between devices by JAX's collectives and lax.ppermute only.
A program may use at most 128 MiB of HBM per device.

v0:
```python
import jax
import jax.numpy as jnp
from jax import lax
from jax.sharding import PartitionSpec as P

TILE_F = 2
TILE_H = 4
TILE_W = 4


EPS = 1e-06


def extended(x, sides, width):
    for axis, dim in sides:
        peers, length = (lax.axis_size(axis), x.shape[dim])
        up = [(i, (i + 1) % peers) for i in range(peers - 1)]
        down = [(j, i) for i, j in up]
        last = lax.slice_in_dim(x, length - width, length, axis=dim)
        first = lax.slice_in_dim(x, 0, width, axis=dim)
        before = lax.ppermute(last, axis, up)
        after = lax.ppermute(first, axis, down)
        x = jnp.concatenate([before, x, after], axis=dim)
    return x


def normalize(raw_values, gain_vector, head_count):
    full_shape = raw_values.shape
    head_size = gain_vector.shape[0]
    split_values = raw_values.astype(jnp.float32).reshape(full_shape[:-1] + (head_count, head_size))
    inverse = lax.rsqrt(jnp.mean(split_values * split_values, axis=-1, keepdims=True) + EPS)
    scaled = (split_values * inverse * gain_vector).reshape(full_shape).astype(jnp.bfloat16)
    return (scaled, split_values, inverse)


def norm_backward(grad_out, split_values, inverse, gain_vector):
    full_shape = grad_out.shape
    grad_split = grad_out.reshape(split_values.shape)
    weighted = grad_split * gain_vector
    inner_mean = jnp.mean(weighted * split_values, axis=-1, keepdims=True)
    grad_in = inverse * weighted - split_values * (inverse * inverse * inverse) * inner_mean
    gain_term = jnp.sum(
        (grad_split * split_values * inverse).reshape(-1, gain_vector.shape[0]), axis=0
    )
    return (grad_in.reshape(full_shape), gain_term)


def head_grads(query_head, key_head, value_head, grad_head, allowed):
    score_scale = query_head.shape[-1] ** (-0.5)
    scores = jnp.dot(query_head, key_head.T, preferred_element_type=jnp.float32) * score_scale
    scores = jnp.where(allowed, scores, -1e30)
    peak_score = jnp.max(scores, axis=-1, keepdims=True)
    weights = jnp.exp(scores - peak_score)
    weights = weights / jnp.sum(weights, axis=-1, keepdims=True)
    weights_low = weights.astype(jnp.bfloat16)
    output = jnp.dot(weights_low, value_head, preferred_element_type=jnp.float32)
    delta_row = jnp.sum(grad_head.astype(jnp.float32) * output, axis=-1, keepdims=True)
    value_part = jnp.dot(weights_low.T, grad_head, preferred_element_type=jnp.float32)
    prob_grad = jnp.dot(grad_head, value_head.T, preferred_element_type=jnp.float32)
    score_grad = (weights * (prob_grad - delta_row)).astype(jnp.bfloat16)
    query_part = jnp.dot(score_grad, key_head, preferred_element_type=jnp.float32) * score_scale
    key_part = jnp.dot(score_grad.T, query_head, preferred_element_type=jnp.float32) * score_scale
    return (query_part, key_part, value_part)


def split_heads(matrix, head_count):
    return matrix.reshape(matrix.shape[0], head_count, -1).transpose(1, 0, 2)


def merge_heads(stacked):
    return stacked.transpose(1, 0, 2).reshape(stacked.shape[1], -1)


def tile_window(first_tiles, second_tiles, extent):
    within = jnp.abs(first_tiles[:, None, 0] - second_tiles[None, :, 0]) <= extent[0]
    within = within & (jnp.abs(first_tiles[:, None, 1] - second_tiles[None, :, 1]) <= extent[1])
    return within & (jnp.abs(first_tiles[:, None, 2] - second_tiles[None, :, 2]) <= extent[2])


def allowed_mask(query_tiles, key_tiles, key_valid, text_valid, extent):
    within = tile_window(query_tiles, key_tiles, extent)
    video_mask = within & key_valid[None, :]
    text_mask = jnp.broadcast_to(text_valid[None, :], (query_tiles.shape[0], text_valid.shape[0]))
    return jnp.concatenate([video_mask, text_mask], axis=1)


def attend_all(
    query_flat,
    key_flat,
    value_flat,
    grad_flat,
    extents,
    query_tiles,
    key_tiles,
    key_valid,
    text_valid,
):
    head_count = extents.shape[0]

    def per_head(operands):
        query_head, key_head, value_head, grad_head, extent = operands
        allowed = allowed_mask(query_tiles, key_tiles, key_valid, text_valid, extent)
        return head_grads(query_head, key_head, value_head, grad_head, allowed)

    grad_query, grad_keys, grad_values = lax.map(
        per_head,
        (
            split_heads(query_flat, head_count),
            split_heads(key_flat, head_count),
            split_heads(value_flat, head_count),
            split_heads(grad_flat, head_count),
            extents,
        ),
    )
    return (merge_heads(grad_query), merge_heads(grad_keys), merge_heads(grad_values))


def tile_coords(frame_index, row_index, column_index):
    full_shape = (frame_index.shape[0], row_index.shape[0], column_index.shape[0])
    pieces = [
        jnp.broadcast_to((frame_index // TILE_F)[:, None, None], full_shape),
        jnp.broadcast_to((row_index // TILE_H)[None, :, None], full_shape),
        jnp.broadcast_to((column_index // TILE_W)[None, None, :], full_shape),
    ]
    return jnp.stack(pieces, axis=-1).reshape(-1, 3)


def fold_axis(array, axis_number, width, inner_count):
    owned = lax.slice_in_dim(array, 2 * width, 2 * width + inner_count, axis=axis_number)
    lower = lax.slice_in_dim(array, 0, width, axis=axis_number)
    upper = lax.slice_in_dim(
        array, inner_count + 3 * width, inner_count + 4 * width, axis=axis_number
    )
    low_pad = [(0, 0)] * array.ndim
    high_pad = [(0, 0)] * array.ndim
    low_pad[axis_number] = (0, inner_count - width)
    high_pad[axis_number] = (inner_count - width, 0)
    return owned + jnp.pad(lower, low_pad) + jnp.pad(upper, high_pad)


def local(
    queries, keys, values, text_keys, text_values, gain_q, gain_k, window_ext, text_len, out_grad
):
    head_count = window_ext.shape[0]
    frame_count, row_count, column_count, feature_count = queries.shape[1:]
    text_count = text_keys.shape[1]
    frame_base = lax.axis_index("tm") * frame_count
    row_base = lax.axis_index("height") * row_count
    total_frames = frame_count * lax.axis_size("tm")
    total_rows = row_count * lax.axis_size("height")
    query_norm, query_split, query_inverse = normalize(queries[0], gain_q, head_count)
    key_norm, key_split, key_inverse = normalize(keys[0], gain_k, head_count)
    stacked = jnp.stack([key_norm, values[0]])
    rowed = extended(stacked, (("height", 2),), TILE_H)
    beside_all = extended(rowed, (("tm", 1),), TILE_F)
    frames_wide = frame_count + 2 * TILE_F
    rows_wide = row_count + 2 * TILE_H
    column_index = jnp.arange(column_count)
    query_frames = frame_base + jnp.arange(frame_count)
    query_rows = row_base + jnp.arange(row_count)
    key_frames = frame_base - TILE_F + jnp.arange(frames_wide)
    key_rows = row_base - TILE_H + jnp.arange(rows_wide)
    query_tiles = tile_coords(query_frames, query_rows, column_index)
    key_tiles = tile_coords(key_frames, key_rows, column_index)
    frame_valid = (key_frames >= 0) & (key_frames < total_frames)
    row_valid = (key_rows >= 0) & (key_rows < total_rows)
    key_valid = jnp.broadcast_to(
        frame_valid[:, None, None] & row_valid[None, :, None],
        (frames_wide, rows_wide, column_count),
    ).reshape(-1)
    text_valid = jnp.arange(text_count) < text_len[0]
    key_all = jnp.concatenate([beside_all[0].reshape(-1, feature_count), text_keys[0]], axis=0)
    value_all = jnp.concatenate([beside_all[1].reshape(-1, feature_count), text_values[0]], axis=0)
    query_flat = query_norm.reshape(-1, feature_count)
    grad_flat = out_grad[0].reshape(-1, feature_count)
    video_count = frames_wide * rows_wide * column_count
    grad_query, grad_keys, grad_values = attend_all(
        query_flat,
        key_all,
        value_all,
        grad_flat,
        window_ext,
        query_tiles,
        key_tiles,
        key_valid,
        text_valid,
    )
    grads = jnp.stack([grad_keys[:video_count], grad_values[:video_count]]).reshape(
        2, frames_wide, rows_wide, column_count, feature_count
    )
    returned = extended(grads, (("tm", 1),), TILE_F)
    partial_sum = fold_axis(returned, 1, TILE_F, frame_count)
    returned_rows = extended(partial_sum, (("height", 2),), TILE_H)
    owned = fold_axis(returned_rows, 2, TILE_H, row_count)
    key_own = owned[0]
    value_own = owned[1]
    text_key_part = grad_keys[video_count:]
    text_value_part = grad_values[video_count:]
    query_full = grad_query.reshape(frame_count, row_count, column_count, feature_count)
    query_out, query_gain = norm_backward(query_full, query_split, query_inverse, gain_q)
    key_out, key_gain = norm_backward(key_own, key_split, key_inverse, gain_k)
    gain_terms = jnp.stack([query_gain, key_gain])
    text_key_sum, text_value_sum = lax.psum((text_key_part, text_value_part), ("tm", "height"))
    gain_total = lax.psum(gain_terms, ("dp", "tm", "height"))
    return (
        query_out.astype(jnp.bfloat16)[None],
        key_out.astype(jnp.bfloat16)[None],
        value_own.astype(jnp.bfloat16)[None],
        text_key_sum[None],
        text_value_sum[None],
        gain_total,
    )


def solution(mesh):
    return jax.shard_map(
        local,
        mesh=mesh,
        in_specs=(
            P("dp", "tm", "height", None, None),
            P("dp", "tm", "height", None, None),
            P("dp", "tm", "height", None, None),
            P("dp", None, None),
            P("dp", None, None),
            P(),
            P(),
            P(),
            P("dp"),
            P("dp", "tm", "height", None, None),
        ),
        out_specs=(
            P("dp", "tm", "height", None, None),
            P("dp", "tm", "height", None, None),
            P("dp", "tm", "height", None, None),
            P("dp", None, None),
            P("dp", None, None),
            P(),
        ),
        check_vma=False,
    )
```

profile of v0, /device:TPU:0, one launch (start us, length us, event | category | flops | bytes accessed | tf_op | source)
XLA Modules:
  0.0 574.4 jit_solution(11806287769408357860)
XLA Ops:
  12.3 2.4 collective-permute-start
  16.1 2.3 collective-permute-done.1
  21.0 6.0 %collective-permute-start.2 = (bf16[2,2,16,8,1536]{4,3,2,1,0:T(8,128)(2,1)}, bf16[2,2,16,8,1536]{4,3,2,1,0:T(8,128)(2,1)}, u32[]{:S(2)}, u32[]{:S(2)}) collective-permute-start(bf16[2,2,16,8,1536]{4,3,2,1,0:T(8,128)(2,1)} %pad_maximum_fusion.1), channel_id=1, source_target_pairs={{0,2},{2,4},{4,6},{6,8},{8,10},{10,12},{12,14},{1,3},{3,5},{5,7},{... | collective-permute-start | bytes 4718600 | tf_op jit(solution)/shard_map/ppermute | solution.py:21
  33.6 1.9 copy.74
  37.0 1.7 copy.76
  40.6 18.4 %collective-permute-done.3 = bf16[2,2,16,8,1536]{4,3,2,1,0:T(8,128)(2,1)} collective-permute-done((bf16[2,2,16,8,1536]{4,3,2,1,0:T(8,128)(2,1)}, bf16[2,2,16,8,1536]{4,3,2,1,0:T(8,128)(2,1)}, u32[]{:S(2)}, u32[]{:S(2)}) %collective-permute-start.3) | collective-permute-done | bytes 1572896 | tf_op jit(solution)/shard_map/ppermute | solution.py:22
  59.0 33.9 %collective-permute-done.2 = bf16[2,2,16,8,1536]{4,3,2,1,0:T(8,128)(2,1)} collective-permute-done((bf16[2,2,16,8,1536]{4,3,2,1,0:T(8,128)(2,1)}, bf16[2,2,16,8,1536]{4,3,2,1,0:T(8,128)(2,1)}, u32[]{:S(2)}, u32[]{:S(2)}) %collective-permute-start.2) | collective-permute-done | bytes 1572896 | tf_op jit(solution)/shard_map/ppermute | solution.py:21
  92.8 3.0 pad_maximum_fusion
  95.8 2.8 fusion.59
  98.6 4.2 concatenate.31
  102.7 1.9 maximum_bitcast_fusion.1
  104.6 2.4 copy.80
  107.1 4.2 concatenate.28
  111.2 1.9 maximum_bitcast_fusion
  113.2 2.5 copy.78
  115.7 173.7 %while.15 = (s32[]{:T(128)}, f32[12,128,128]{2,0,1:T(8,128)S(1)}, f32[12,1024,128]{1,2,0:T(8,128)}, f32[12,1024,128]{1,2,0:T(8,128)}, s32[128,3]{0,1:T(4,128)S(1...) while((s32[]{:T(128)}, f32[12,128,128]{2,0,1:T(8,128)S(1)}, ...), condition=%wide.region_6.7_spmd.clone, body=%wide.region_2.6_spmd.clone.sunk | while | flops 204930944 | bytes 8207186 | solution.py:105
  117.2 2.3 fusion.92
  127.4 1.9 fusion.98
  131.7 2.3 fusion.92
  141.9 1.9 fusion.98
  146.2 2.3 fusion.92
  156.4 1.9 fusion.98
  160.6 2.3 fusion.92
  170.9 1.9 fusion.98
  175.1 2.3 fusion.92
  185.3 1.9 fusion.98
  189.6 2.3 fusion.92
  199.8 1.9 fusion.98
  204.0 2.3 fusion.92
  214.3 1.9 fusion.98
  218.5 2.3 fusion.92
  228.7 1.9 fusion.98
  233.0 2.3 fusion.92
  243.2 1.9 fusion.98
  247.5 2.3 fusion.92
  257.7 1.9 fusion.98
  261.9 2.3 fusion.92
  272.2 1.9 fusion.98
  276.4 2.3 fusion.92
  286.6 1.9 fusion.98
  289.4 5.2 slice.118
  294.5 6.6 %copy.85 = f32[768,12,128]{2,1,0:T(8,128)} copy(f32[768,12,128]{0,2,1:T(8,128)} %slice.118) | data formatting | bytes 9437184 | tf_op jit(solution)/shard_map/slice | solution.py:188
  301.2 6.8 %stack.31 = f32[1,6,16,8,1536]{4,3,2,1,0:T(8,128)} reshape(f32[768,12,128]{2,1,0:T(8,128)} %copy.85) | data formatting | bytes 9437184 | tf_op jit(solution)/shard_map/stack | solution.py:188
  307.9 4.9 slice.119
  312.8 6.6 %copy.87 = f32[768,12,128]{2,1,0:T(8,128)} copy(f32[768,12,128]{0,2,1:T(8,128)} %slice.119) | data formatting | bytes 9437184 | tf_op jit(solution)/shard_map/slice | solution.py:188
  319.4 6.8 %stack.32 = f32[1,6,16,8,1536]{4,3,2,1,0:T(8,128)} reshape(f32[768,12,128]{2,1,0:T(8,128)} %copy.87) | data formatting | bytes 9437184 | tf_op jit(solution)/shard_map/stack | solution.py:188
  326.1 2.8 constant_dynamic-update-slice_fusion.2
  330.2 3.4 fusion.58
  333.6 2.2 copy-done
  335.8 4.8 collective-permute-start.4
  342.0 1.7 copy.88
  345.2 2.7 slice.128
  347.9 2.7 slice.129
  350.6 141.3 %collective-permute-done.4 = f32[2,2,16,8,1536]{4,3,2,1,0:T(8,128)S(1)} collective-permute-done((f32[2,2,16,8,1536]{4,3,2,1,0:T(8,128)}, f32[2,2,16,8,1536]{4,3,2,1,0:T(8,128)S(1)}, u32[]{:S(2)}, u32[]{:S(2)}) %collective-permute-start.4) | collective-permute-done | bytes 3145760 | tf_op jit(solution)/shard_map/ppermute | solution.py:21
  491.9 1.7 copy-done.10
  493.5 4.8 fusion.41
  499.7 2.2 collective-permute-start.6
  508.7 1.6 copy.83
  510.3 2.2 reshape_reshape_reshape.3
  512.6 2.6 fusion.53
  515.2 3.0 copy.89
  518.3 3.0 copy.90
  521.3 1.6 fusion.42
  526.0 41.6 %psum.23 = f32[2,128]{1,0:T(2,128)} all-reduce(f32[2,128]{1,0:T(2,128)S(1)} %pad_maximum_fusion.3), channel_id=1, replica_groups=mesh['dp'=2,'tm'=8,'height'=2] {'dp','tm','height'}, use_global_device_ids=true, to_apply=%region_13.14 | all-reduce | flops 256 | bytes 2048 | tf_op jit(solution)/shard_map/psum | solution.py:204
  (317 shorter events, 156.7 us)
Async XLA Ops:
  7.2 11.2 %copy-start.8 = (bf16[1,2,8,8,1536]{4,3,2,1,0:T(8,128)(2,1)S(1)}, bf16[1,2,8,8,1536]{4,3,2,1,0:T(8,128)(2,1)}, u32[]{:S(2)}) copy-start(bf16[1,2,8,8,1536]{4,3,2,1,0:T(8,128)(2,1)} %param.14) | copy-start | bytes 1179652
  7.2 508.1 %all-reduce.5.cloned.1.call-start = ((), (), s32[]{:S(2)}) async-start(), calls=%async_computation | async-start | bytes 6291456 | tf_op jit(solution)/shard_map/psum | solution.py:203
  7.9 6.9 %copy-start.18 = (f32[1536]{0:T(1024)}, f32[1536]{0:T(1024)S(1)}, u32[]{:S(2)}) copy-start(f32[1536]{0:T(1024)S(1)} %broadcast_bitcast_fusion.1) | copy-start | bytes 18436
  9.9 17.8 %copy-start.11 = (f32[2,8,8,12]{2,3,1,0:T(8,128)}, f32[2,8,8,12]{2,3,1,0:T(8,128)S(1)}, u32[]{:S(2)}) copy-start(f32[2,8,8,12]{2,3,1,0:T(8,128)S(1)} %get-tuple-element.218) | copy-start | bytes 18436
  9.9 17.8 %copy-start.9 = (bf16[1,2,8,8,1536]{4,3,2,1,0:T(8,128)(2,1)S(1)}, bf16[1,2,8,8,1536]{4,3,2,1,0:T(8,128)(2,1)}, u32[]{:S(2)}) copy-start(bf16[1,2,8,8,1536]{4,3,2,1,0:T(8,128)(2,1)} %param.12) | copy-start | bytes 1179652
  12.3 3.8 collective-permute-start
  14.8 3.6 collective-permute-start.1
  18.4 10.6 %copy-start.13 = (bf16[2,2,4,8,1536]{4,3,2,1,0:T(8,128)(2,1)}, bf16[2,2,4,8,1536]{4,3,2,1,0:T(8,128)(2,1)S(1)}, u32[]{:S(2)}) copy-start(bf16[2,2,4,8,1536]{4,3,2,1,0:T(8,128)(2,1)S(1)} %collective-permute-done.1) | copy-start | bytes 1179652
  19.7 39.2 %collective-permute-start.3 = (bf16[2,2,16,8,1536]{4,3,2,1,0:T(8,128)(2,1)}, bf16[2,2,16,8,1536]{4,3,2,1,0:T(8,128)(2,1)}, u32[]{:S(2)}, u32[]{:S(2)}) collective-permute-start(bf16[2,2,16,8,1536]{4,3,2,1,0:T(8,128)(2,1)} %pad_maximum_fusion.1), channel_id=1, source_target_pairs={{2,0},{4,2},{6,4},{8,6},{10,8},{12,10},{14,12},{3,1},{5,3},{7,5},{... | collective-permute-start | bytes 4718600 | tf_op jit(solution)/shard_map/ppermute | solution.py:22
  21.0 71.8 %collective-permute-start.2 = (bf16[2,2,16,8,1536]{4,3,2,1,0:T(8,128)(2,1)}, bf16[2,2,16,8,1536]{4,3,2,1,0:T(8,128)(2,1)}, u32[]{:S(2)}, u32[]{:S(2)}) collective-permute-start(bf16[2,2,16,8,1536]{4,3,2,1,0:T(8,128)(2,1)} %pad_maximum_fusion.1), channel_id=1, source_target_pairs={{0,2},{2,4},{4,6},{6,8},{8,10},{10,12},{12,14},{1,3},{3,5},{5,7},{... | collective-permute-start | bytes 4718600 | tf_op jit(solution)/shard_map/ppermute | solution.py:21
  27.9 10.8 %copy-start.2 = (f32[128,12,128]{2,1,0:T(8,128)}, f32[128,12,128]{2,1,0:T(8,128)S(1)}, u32[]{:S(2)}) copy-start(f32[128,12,128]{2,1,0:T(8,128)S(1)} %reshape.281) | copy-start | bytes 2359300
  29.0 0.7 copy-start.14
  29.8 8.9 %copy-start.15 = (f32[2,8,8,12]{3,2,1,0:T(8,128)}, f32[2,8,8,12]{3,2,1,0:T(8,128)S(1)}, u32[]{:S(2)}) copy-start(f32[2,8,8,12]{3,2,1,0:T(8,128)S(1)} %copy.91) | copy-start | bytes 18436
  32.2 6.5 %copy-start.22 = (f32[128]{0:T(128)S(1)}, f32[128]{0:T(128)}, u32[]{:S(2)}) copy-start(f32[128]{0:T(128)} %param.17) | copy-start | bytes 1540
  113.2 2.5 copy-start.5
  113.2 2.5 copy-start.20
  113.2 2.5 copy-start.21
  289.4 5.2 copy-start.6
  326.1 3.8 copy-start.1
  330.2 5.6 copy-start
  335.8 156.0 %collective-permute-start.4 = (f32[2,2,16,8,1536]{4,3,2,1,0:T(8,128)}, f32[2,2,16,8,1536]{4,3,2,1,0:T(8,128)S(1)}, u32[]{:S(2)}, u32[]{:S(2)}) collective-permute-start(f32[2,2,16,8,1536]{4,3,2,1,0:T(8,128)} %get-tuple-element.207), channel_id=1, source_target_pairs={{0,2},{2,4},{4,6},{6,8},{8,10},{10,12},{12,14},{1,3},{3,5},{5,7},{... | collective-permute-start | bytes 9437192 | tf_op jit(solution)/shard_map/ppermute | solution.py:21
  340.7 152.9 %collective-permute-start.5 = (f32[2,2,16,8,1536]{4,3,2,1,0:T(8,128)}, f32[2,2,16,8,1536]{4,3,2,1,0:T(8,128)}, u32[]{:S(2)}, u32[]{:S(2)}) collective-permute-start(f32[2,2,16,8,1536]{4,3,2,1,0:T(8,128)} %get-tuple-element.208), channel_id=1, source_target_pairs={{2,0},{4,2},{6,4},{8,6},{10,8},{12,10},{14,12},{3,1},{5,3},{7,5},{... | collective-permute-start | bytes 9437192 | tf_op jit(solution)/shard_map/ppermute | solution.py:22
  491.9 1.7 copy-start.10
  498.4 4.8 copy-start.3
  498.4 4.8 copy-start.7
  498.4 4.8 copy-start.16
  498.4 4.8 copy-start.23
  499.7 21.6 %collective-permute-start.6 = (f32[2,2,4,8,1536]{4,3,2,1,0:T(8,128)}, f32[2,2,4,8,1536]{4,3,2,1,0:T(8,128)}, u32[]{:S(2)}, u32[]{:S(2)}) collective-permute-start(f32[2,2,4,8,1536]{4,3,2,1,0:T(8,128)} %get-tuple-element.211), channel_id=1, source_target_pairs={{0,1},{2,3},{4,5},{6,7},{8,9},{10,11},{12,13},{14,15},{16,17},{18,... | collective-permute-start | bytes 2359304 | tf_op jit(solution)/shard_map/ppermute | solution.py:21
  501.9 19.4 %collective-permute-start.7 = (f32[2,2,4,8,1536]{4,3,2,1,0:T(8,128)}, f32[2,2,4,8,1536]{4,3,2,1,0:T(8,128)}, u32[]{:S(2)}, u32[]{:S(2)}) collective-permute-start(f32[2,2,4,8,1536]{4,3,2,1,0:T(8,128)} %get-tuple-element.212), channel_id=1, source_target_pairs={{1,0},{3,2},{5,4},{7,6},{9,8},{11,10},{13,12},{15,14},{17,16},{19,... | collective-permute-start | bytes 2359304 | tf_op jit(solution)/shard_map/ppermute | solution.py:22
  521.3 1.7 copy-start.4
  521.3 1.7 copy-start.24
  521.3 2.8 copy-start.12
  521.3 2.8 copy-start.17
  521.3 2.8 copy-start.19
  523.3 2.7 copy-start.25
Sparse Core Ops, SparseCore 0:
  350.7 164.4 all-reduce.4
where the time goes:
time: 579 us; the launch traced here: 574 us
  waiting for transfers between devices  196 us (34%)
  local copies, waits for them, and re-layouts  139 us (24%)
  matrix products  95.2 us (16%)
  other arithmetic  66.2 us (11%)
  blocking collectives  41.6 us (7%)
  starting transfers between devices  20.6 us (4%)
  between operations  14.5 us (3%)
    ppermute x4, waiting for transfers between devices, extended(): before = lax.ppermute(last, axis, up)  175 us
    psum x1, blocking collectives, local(): gain_total = lax.psum(gain_terms, ('dp', 'tm', 'height'))  41.6 us
    dynamic_update_slice x36, local copies, waits for them, and re-layouts, attend_all(): lax.map(per_head, (split_heads(query_flat, head_count), split_heads(key_f...  29.8 us
    and x12, other arithmetic, allowed_mask(): video_mask = within & key_valid[None, :]  27.4 us
    unnamed x61, local copies, waits for them, and re-layouts  24.1 us
    dot_general x12, matrix products, head_grads(): jnp.dot(weights_low.T, grad_head, preferred_element_type=jnp.float32)  22.7 us
    ppermute x4, waiting for transfers between devices, extended(): after = lax.ppermute(first, axis, down)  20.7 us
    dot_general x12, matrix products, head_grads(): jnp.dot(weights_low, value_head, preferred_element_type=jnp.float32)  15.8 us
  transfers between devices with their start and end apart: 9, of which 5 were waited for; matrix products, arithmetic and copies ran while one was open for 8% of the time, Pallas kernels for 0%

commit v1 on v0

v1 whole, which is shorter than its diff:
```python
import jax
import jax.numpy as jnp
import numpy as np
from jax import lax
from jax.experimental import pallas as pl
from jax.experimental.pallas import tpu as pltpu
from jax.sharding import PartitionSpec as P


TILE_F = 2
TILE_H = 4
TILE_W = 4
EPS = 1e-06
HIDDEN = -1e30
LOG2E = 1.4426950408889634


F32 = jnp.float32
BF16 = jnp.bfloat16
VMEM = pl.BlockSpec(memory_space=pltpu.VMEM)
HBM = pl.BlockSpec(memory_space=pltpu.HBM)


def call(kernel, scalars, operands, outputs, scratch=(), aliases=None, limit=24):
    spec = {"vmem": VMEM, "hbm": HBM, "out": VMEM}
    held = [pltpu.with_memory_space_constraint(x, pltpu.VMEM) if space == "vmem" else x for x, space in operands]
    return pl.pallas_call(
        kernel,
        grid_spec=pltpu.PrefetchScalarGridSpec(
            num_scalar_prefetch=len(scalars),
            grid=(),
            in_specs=[spec[space] for _, space in operands],
            out_specs=[spec[space] for _, _, space in outputs],
            scratch_shapes=list(scratch),
        ),
        out_shape=[
            pltpu.VMEM(shape, dtype) if space == "vmem" else jax.ShapeDtypeStruct(shape, dtype)
            for shape, dtype, space in outputs
        ],
        input_output_aliases=aliases or {},
        compiler_params=pltpu.CompilerParams(vmem_limit_bytes=limit << 20),
    )(*scalars, *held)


def dot(x, y, dims):
    return lax.dot_general(x, y, ((dims[:1], dims[1:]), ((), ())), preferred_element_type=F32)


def pack(place, arrays, groups):
    tokens, features = arrays[0].shape
    width = features // 4
    total = sum(len(picked) for _, picked in groups)

    def kernel(place_ref, *refs):
        sems = refs[-1]
        copies = []
        for out_ref, (j, picked) in zip(refs[len(arrays):-1], groups):
            start = pl.multiple_of((place_ref[0] ^ j) * width, 128)
            for i, n in enumerate(picked):
                copies.append(
                    pltpu.make_async_copy(refs[n].at[:, pl.ds(start, width)], out_ref.at[i], sems.at[len(copies)])
                )
        for copy in copies:
            copy.start()
        for copy in copies:
            copy.wait()

    return call(
        kernel, [place], [(x, "hbm") for x in arrays],
        [((len(picked), tokens, width), arrays[0].dtype, "vmem") for _, picked in groups],
        [pltpu.SemaphoreType.DMA((total,))],
    )


def stage(place, texts, gains, masks):
    rows, features = texts[0].shape
    width = features // 4

    def kernel(place_ref, tk, tv, gq, gk, mask, text_ref, gain_ref, mask_ref, sems):
        columns = pl.ds(pl.multiple_of(place_ref[0] * width, 128), width)
        pairs = [(tk.at[:, columns], text_ref.at[0]), (tv.at[:, columns], text_ref.at[1])]
        pairs += [(gq, gain_ref.at[0:1]), (gk, gain_ref.at[1:2]), (mask, mask_ref)]
        copies = [pltpu.make_async_copy(x, y, sems.at[i]) for i, (x, y) in enumerate(pairs)]
        for copy in copies:
            copy.start()
        for copy in copies:
            copy.wait()

    return call(
        kernel, [place], [(x, "hbm") for x in (*texts, *gains, masks)],
        [((2, rows, width), texts[0].dtype, "vmem"), ((2, 128), F32, "vmem"), (masks.shape, F32, "vmem")],
        [pltpu.SemaphoreType.DMA((5,))],
    )


def unpack(place, pieces):
    count, rows, width = pieces[0].shape

    def kernel(place_ref, *refs):
        sems = refs[-1]
        copies = []
        for j in range(4):
            start = pl.multiple_of((place_ref[0] ^ j) * width, 128)
            for i in range(count):
                copies.append(
                    pltpu.make_async_copy(refs[j].at[i], refs[4 + i].at[:, pl.ds(start, width)], sems.at[len(copies)])
                )
        for copy in copies:
            copy.start()
        for copy in copies:
            copy.wait()

    return call(
        kernel, [place], [(x, "vmem") for x in pieces],
        [((rows, 4 * width), pieces[0].dtype, "hbm")] * count,
        [pltpu.SemaphoreType.DMA((4 * count,))],
    )


def unit(x):
    x = x.astype(F32)
    inverse = lax.rsqrt(jnp.mean(x * x, axis=-1, keepdims=True) + EPS)
    return x * inverse, inverse


def spatial(half, columns, slot):
    tile_rows, tile_cols = half // TILE_H, columns // TILE_W
    n = np.arange(2 * slot)
    row = (n // slot) * tile_rows + ((n // columns) % half) // TILE_H
    col = (n % columns) // TILE_W
    space = 2 * tile_rows * tile_cols
    code = np.arange(128) % space
    rows_off = np.abs(row[:, None] - code[None, :] // tile_cols)
    cols_off = np.abs(col[:, None] - code[None, :] % tile_cols)
    hot = ((row * tile_cols + col)[:, None] == np.arange(128)[None, :]) * 1.0
    return jnp.asarray(np.stack([rows_off, cols_off, hot]), F32), space


def hidden(seen):
    return jnp.where(seen, 0.0, HIDDEN).astype(BF16)


def spots(g, slot, near, far):
    a, b = g >> 1, g & 1
    a_base, b_base = jnp.where(a == 0, far, near), jnp.where(a == 0, near, far)
    halo = [a_base + b * slot, a_base + (1 - b) * slot, b_base + b * slot, b_base + (1 - b) * slot]
    return [(g ^ j) * slot for j in range(4)], halo


def attention(place, window_ext, text_len, near, kv, qd, halos, words, masks, space, gain, chunks):
    _, slot, width = near[0].shape
    heads = width // 128
    text_count = words.shape[1]
    tile = 2 * slot
    video = 4 * tile
    chunk = text_count // chunks
    scale = 128 ** -0.5

    def kernel(place_ref, ext_ref, len_ref, *refs):
        n0, n1, kv2, kv3, qd2, qd3, ha0, ha1, hb0, hb1, text_ref, mask_ref, gain_ref = refs[:13]
        oqs, own, ogain = refs[13:17], refs[17], refs[18]
        messages = refs[19:19 + chunks]
        kn, vs, kx, qn, grads, qx, qr, dk, dv, ends = refs[19 + chunks:]
        g, p, last = place_ref[0], place_ref[1], place_ref[2]
        gq, gk = gain_ref[0:1, :], gain_ref[1:2, :]
        at = lambda start: pl.ds(pl.multiple_of(start, slot), slot)
        own_at, halo_at = spots(g, slot, 0, 3 * tile)
        for t in range(2):
            hot = mask_ref[2] if t == 0 else pltpu.roll(mask_ref[2], space, 1)
            qn[t * tile:(t + 1) * tile, 128:] = hot.astype(BF16)
        lane_tile = lax.broadcasted_iota(jnp.int32, (1, 128), 1) // space
        word = lax.broadcasted_iota(jnp.int32, (text_count, 128), 0)
        kn[video:, 128:] = hidden(word < len_ref[0])
        ogain[...] = jnp.zeros((2, 128), F32)
        for out in messages:
            out[2 * chunk:, :] = jnp.zeros((8, width), F32)

        def one_head(h, _):
            lanes = pl.ds(pl.multiple_of(h * 128, 128), 128)
            head = heads * g + h
            e0, e1, e2 = ext_ref[0, head], ext_ref[1, head].astype(F32), ext_ref[2, head].astype(F32)

            sources = [(r, start + tile) for r, start in zip((n0, n1, kv2, kv3), own_at)]
            sources += list(zip((ha0, ha1, hb0, hb1), halo_at))
            for r, start in sources:
                hat, _ = unit(r[0, :, lanes])
                kx[at(start), :] = hat
                kn[at(start), :128] = (hat * gk).astype(BF16)
                vs[at(start), :] = r[1, :, lanes]
            kn[video:, :128] = text_ref[0, :, lanes]
            vs[video:, :] = text_ref[1, :, lanes]
            for r, i, start in zip((n0, n1, qd2, qd3), (2, 2, 0, 0), own_at):
                hat, inverse = unit(r[i, :, lanes])
                qx[at(start), :] = hat
                qr[at(start), :] = jnp.broadcast_to(inverse, hat.shape)
                qn[at(start), :128] = (hat * gq).astype(BF16)
                grads[at(start), :] = r[i + 1, :, lanes]
            close = (mask_ref[0] <= e1) & (mask_ref[1] <= e2)
            for block in range(4):
                framed = jnp.abs(block - 1 - lane_tile) <= e0
                if block == 0:
                    framed = framed & (p > 0)
                if block == 3:
                    framed = framed & (p < last)
                kn[block * tile:(block + 1) * tile, 128:] = hidden(close & framed)

            words = slice(video, video + text_count)
            parts = [(slice(t * tile, (t + 3) * tile), words) for t in range(2)]
            rows = [slice(t * tile, (t + 1) * tile) for t in range(2)]

            def softmax(scores):
                top = jnp.maximum(*[jnp.max(s, axis=0, keepdims=True) for s in scores])
                powers = [jnp.exp2((s - top) * (scale * LOG2E)) for s in scores]
                share = 1.0 / sum(jnp.sum(e, axis=0, keepdims=True) for e in powers)
                probs = [e * share for e in powers]
                return top, share, probs, [x.astype(BF16) for x in probs]

            scores = [[dot(kn[x, :], qn[rows[t], :], (1, 1)) for x in parts[t]] for t in range(2)]
            soft = [softmax(scores[t]) for t in range(2)]
            for t in range(2):
                top, share, probs, low = soft[t]
                query, grad = qn[rows[t], :128], grads[rows[t], :]
                attn = sum(dot(vs[x, :], w, (0, 0)) for x, w in zip(parts[t], low))
                prob_grad = [dot(vs[x, :], grad, (1, 1)) for x in parts[t]]
                delta = jnp.sum(grad.astype(F32).T * attn, axis=0, keepdims=True)
                message = messages[chunks - 1] if t == 0 else messages[1]
                for i, number in enumerate((top, share, delta)):
                    for side in range(2):
                        row = 2 * chunk + 2 * i + side
                        message[row:row + 1, lanes] = number[:, side * 128:side * 128 + 128]
                score_grad = [(w * (y - delta)).astype(BF16) for w, y in zip(probs, prob_grad)]
                dqn = sum(dot(kn[x, :128], s, (0, 0)) for x, s in zip(parts[t], score_grad)).T * scale
                mine = slice((1 - t) * tile, (3 - t) * tile)
                for x, w, s in (
                    (slice(0, 2 * tile), low[0][mine], score_grad[0][mine]),
                    (slice(2 * tile, 2 * tile + text_count), low[1], score_grad[1]),
                ):
                    value_part = dot(w, grad, (1, 0))
                    key_part = dot(s, query, (1, 0)) * scale
                    if t == 0:
                        dv[x, :] = value_part
                        dk[x, :] = key_part
                    else:
                        dv[x, :] += value_part
                        dk[x, :] += key_part
                hat = qx[rows[t], :]
                weighted = dqn * gq
                inner = jnp.mean(weighted * hat, axis=-1, keepdims=True)
                ends[rows[t], :] = (qr[rows[t], :] * (weighted - hat * inner)).astype(BF16)
                ogain[0:1, :] += jnp.sum(dqn * hat, axis=0, keepdims=True)
                around = slice(2 * t * tile, (2 * t + 1) * tile)
                key_part = dot(score_grad[0][around], query, (1, 0)) * scale
                where = slice(3 * t * tile, (3 * t + 1) * tile)
                ogain[1:2, :] += jnp.sum(key_part * kx[where, :], axis=0, keepdims=True)
            ogain[1:2, :] += jnp.sum(dk[:2 * tile, :] * kx[tile:3 * tile, :], axis=0, keepdims=True)

            for j, out in enumerate(oqs):
                out[0, :, lanes] = ends[at(own_at[j]), :]
            own[0, :, lanes] = dk[:2 * tile, :]
            own[1, :, lanes] = dv[:2 * tile, :]
            for d, out in enumerate(messages):
                start = pl.multiple_of(2 * tile + lax.rem(p + d, chunks) * chunk, 8)
                out[:chunk, lanes] = dk[pl.ds(start, chunk), :]
                out[chunk:2 * chunk, lanes] = dv[pl.ds(start, chunk), :]
            return 0

        lax.fori_loop(0, heads, one_head, 0)

    operands = [*near, *kv, *qd, *halos, words, masks, gain]
    return call(
        kernel, [place, window_ext, text_len], [(x, "vmem") for x in operands],
        [((1, slot, width), BF16, "vmem")] * 4
        + [((2, 2 * tile, width), F32, "vmem"), ((2, 128), F32, "vmem")]
        + [((2 * chunk + 8, width), F32, "vmem")] * chunks,
        [
            pltpu.VMEM((video + text_count, 256), BF16),
            pltpu.VMEM((video + text_count, 128), BF16),
            pltpu.VMEM((video, 128), F32),
            pltpu.VMEM((2 * tile, 256), BF16),
            pltpu.VMEM((2 * tile, 128), BF16),
            pltpu.VMEM((2 * tile, 128), F32),
            pltpu.VMEM((2 * tile, 128), F32),
            pltpu.VMEM((2 * tile + text_count, 128), F32),
            pltpu.VMEM((2 * tile + text_count, 128), F32),
            pltpu.VMEM((2 * tile, 128), BF16),
        ],
    )


def edges(place, window_ext, own, messages, near, kv, halos_a, halos_b, masks, gain):
    _, slot, width = near[0].shape
    heads = width // 128
    tile = 2 * slot
    chunk = (messages[0].shape[0] - 8) // 2
    scale = 128 ** -0.5

    def kernel(place_ref, ext_ref, *refs):
        own_ref, before_ref, after_ref, n0, n1, kv2, kv3, ha0, ha1, hb0, hb1 = refs[:11]
        mask_ref, gain_ref, o0, o1, o2, o3 = refs[11:17]
        kn, vs, kx, kr, qn, grads, ends = refs[17:]
        g, p, last = place_ref[0], place_ref[1], place_ref[2]
        gq, gk = gain_ref[0:1, :], gain_ref[1:2, :]
        at = lambda start: pl.ds(pl.multiple_of(start, slot), slot)
        own_at, halo_at = spots(g, slot, 0, tile)
        for t in range(2):
            qn[t * tile:(t + 1) * tile, 128:] = mask_ref[2].astype(BF16)

        def one_head(h, _):
            lanes = pl.ds(pl.multiple_of(h * 128, 128), 128)
            head = heads * g + h
            e0, e1, e2 = ext_ref[0, head], ext_ref[1, head].astype(F32), ext_ref[2, head].astype(F32)
            for r, start in zip((n0, n1, kv2, kv3), own_at):
                hat, inverse = unit(r[0, :, lanes])
                kx[at(start), :] = hat
                kr[at(start), :] = jnp.broadcast_to(inverse, hat.shape)
                kn[at(start), :128] = (hat * gk).astype(BF16)
                vs[at(start), :] = r[1, :, lanes]
            for r, i, start in zip((ha0, ha1, hb0, hb1), (2, 2, 0, 0), halo_at):
                qn[at(start), :128] = (unit(r[i, :, lanes])[0] * gq).astype(BF16)
                grads[at(start), :] = r[i + 1, :, lanes]
            close = (mask_ref[0] <= e1) & (mask_ref[1] <= e2) & (e0 >= 1)
            for t in range(2):
                kn[t * tile:(t + 1) * tile, 128:] = hidden(close & ((p > 0) if t == 0 else (p < last)))
            for t, message in enumerate((before_ref, after_ref)):
                rows = slice(t * tile, (t + 1) * tile)
                top, share, delta = [
                    jnp.concatenate([message[2 * chunk + i:2 * chunk + i + 1, lanes] for i in (n, n + 1)], axis=1)
                    for n in (0, 2, 4)
                ]
                query, grad = qn[rows, :], grads[rows, :]
                probs = jnp.exp2((dot(kn[rows, :], query, (1, 1)) - top) * (scale * LOG2E)) * share
                prob_grad = dot(vs[rows, :], grad, (1, 1))
                score_grad = (probs * (prob_grad - delta)).astype(BF16)
                value_sum = own_ref[1, rows, lanes] + dot(probs.astype(BF16), grad, (1, 0))
                key_sum = own_ref[0, rows, lanes] + dot(score_grad, query[:, :128], (1, 0)) * scale
                hat = kx[rows, :]
                weighted = key_sum * gk
                inner = jnp.mean(weighted * hat, axis=-1, keepdims=True)
                ends[0, rows, :] = (kr[rows, :] * (weighted - hat * inner)).astype(BF16)
                ends[1, rows, :] = value_sum.astype(BF16)
            for j, out in enumerate((o0, o1, o2, o3)):
                out[0, :, lanes] = ends[0, at(own_at[j]), :]
                out[1, :, lanes] = ends[1, at(own_at[j]), :]
            return 0

        lax.fori_loop(0, heads, one_head, 0)

    operands = [own, *messages, *near, *kv, *halos_a, *halos_b, masks, gain]
    return call(
        kernel, [place, window_ext], [(x, "vmem") for x in operands],
        [((2, slot, width), BF16, "vmem")] * 4,
        [
            pltpu.VMEM((2 * tile, 256), BF16),
            pltpu.VMEM((2 * tile, 128), BF16),
            pltpu.VMEM((2 * tile, 128), F32),
            pltpu.VMEM((2 * tile, 128), F32),
            pltpu.VMEM((2 * tile, 256), BF16),
            pltpu.VMEM((2 * tile, 128), BF16),
            pltpu.VMEM((2, 2 * tile, 128), BF16),
        ],
    )


def text_chunk(parts, gains):
    padded, width = parts[0].shape
    rows = padded - 8

    def kernel(*refs):
        sums, tails, out_ref = refs[:len(parts)], refs[len(parts):-1], refs[-1]
        total = sums[0][:rows, :]
        for ref in sums[1:]:
            total = total + ref[:rows, :]
        out_ref[:rows, :] = total.astype(BF16)
        out_ref[rows:, :] = jnp.zeros((8, width), BF16)
        rest = tails[0][...]
        for ref in tails[1:]:
            rest = rest + ref[...]
        for i in range(3):
            part = rest.astype(BF16)
            out_ref[rows + 2 * i:rows + 2 * i + 2, :128] = part
            rest = rest - part.astype(F32)

    return call(kernel, [], [(x, "vmem") for x in parts + gains], [((padded, width), BF16, "vmem")])[0]


def text_columns(place, members, firsts, rests, earlier=None):
    chunks, padded, width = rests[0].shape
    chunks, rows = chunks + 1, (padded - 8) // 2
    shape = (rows * chunks, 4 * width)

    def kernel(place_ref, *refs):
        key_ref, value_ref, gain_ref, hold, sems = refs[len(refs) - 5:]
        gains = refs[4][...] if earlier is not None else jnp.zeros((2, 128), F32)
        copies = []
        for n, j in enumerate(members):
            for d in range(chunks):
                piece = refs[n] if d == 0 else refs[2 + n].at[d - 1]
                start = pl.multiple_of(lax.rem(place_ref[1] + (chunks - d), chunks) * rows, 8)
                for i in range(2):
                    hold[n, i, pl.ds(start, rows), :] = piece[i * rows:(i + 1) * rows].astype(F32)
                tail = piece[2 * rows:, :128].astype(F32)
                gains = gains + (tail[0:2] + tail[2:4] + tail[4:6])
            start = pl.multiple_of((place_ref[0] ^ j) * width, 128)
            for i, out in enumerate((key_ref, value_ref)):
                copies.append(pltpu.make_async_copy(hold.at[n, i], out.at[:, pl.ds(start, width)], sems.at[n, i]))
                copies[-1].start()
        gain_ref[...] = gains
        for copy in copies:
            copy.wait()

    more = [] if earlier is None else [(earlier[2], "vmem"), (earlier[0], "hbm"), (earlier[1], "hbm")]
    return call(
        kernel, [place], [(x, "vmem") for x in (*firsts, *rests)] + more,
        [(shape, F32, "hbm"), (shape, F32, "hbm"), ((2, 128), F32, "vmem" if earlier is None else "out")],
        [pltpu.VMEM((2, 2, rows * chunks, width), F32), pltpu.SemaphoreType.DMA((2, 2))],
        {} if earlier is None else {6: 0, 7: 1},
    )


def local(queries, keys, values, text_keys, text_values, gain_q, gain_k, window_ext, text_len, out_grad):
    head_count = window_ext.shape[0]
    frames, half, columns, features = queries.shape[1:]
    text_count = text_keys.shape[1]
    peers, heights, samples = lax.axis_size("tm"), lax.axis_size("height"), lax.axis_size("dp")
    quads = peers // 2
    assert frames == TILE_F and heights == 2 and peers % 2 == 0 and quads >= 3
    assert features == 128 * head_count and head_count % 4 == 0
    assert half % TILE_H == 0 and columns % TILE_W == 0 and text_count % (8 * quads) == 0
    axes = ("tm", "height")
    me = lax.axis_index("tm")
    quad = me // 2
    member = (me % 2) * 2 + lax.axis_index("height")
    place = jnp.stack([member, quad, jnp.full_like(quad, quads - 1)]).astype(jnp.int32)

    def permute(x, pairs, over=axes):
        return lax.ppermute(x, over, pairs)

    def swap(x, j):
        return permute(x, [(4 * n + m, 4 * n + (m ^ j)) for n in range(quads) for m in range(4)])

    def move(x, step):
        pairs = [(4 * n + m, 4 * (n + step(m // 2)) + m) for n in range(quads) for m in range(4)]
        return permute(x, [(i, j) for i, j in pairs if 0 <= j < 4 * quads])

    def turn(x, d):
        return permute(x, [(4 * n + m, 4 * ((n + d) % quads) + m) for n in range(quads) for m in range(4)])

    out_a, out_b = (lambda a: 2 * a - 1), (lambda a: 1 - 2 * a)
    flat = [x.reshape(-1, features) for x in (keys, values, queries, out_grad)]
    table, space = spatial(half, columns, columns * half * frames)

    near0, near1, kv2, kv3, qd2, qd3 = pack(
        place, flat, [(0, (0, 1, 2, 3)), (1, (0, 1, 2, 3)), (2, (0, 1)), (3, (0, 1)), (2, (2, 3)), (3, (2, 3))]
    )
    kv_in = [swap(kv2, 2), swap(kv3, 3)]
    qd_in = [swap(qd2, 2), swap(qd3, 3)]
    words, gain, masks = stage(
        place, (text_keys[0], text_values[0]), (gain_q.reshape(1, -1), gain_k.reshape(1, -1)), table
    )
    near = [near0, swap(near1, 1)]
    halos_a = [move(near[0], out_a), move(near[1], out_a)]
    kv_halos = [move(kv_in[0], out_b), move(kv_in[1], out_b)]
    qd_halos = [move(qd_in[0], out_b), move(qd_in[1], out_b)]
    ext = window_ext.T

    oq0, oq1, oq2, oq3, own, gains, *texts = attention(
        place, ext, text_len, near, kv_in, qd_in, halos_a + kv_halos, words, masks, space, gain, quads
    )
    text_in = [turn(texts[i], i) for i in range(1, quads)]
    others = [permute(gains, [(n, (n + i) % samples) for n in range(samples)], "dp") for i in range(1, samples)]
    oq_in = [swap(x, j) for x, j in zip((oq1, oq2, oq3), (1, 2, 3))]
    (query_out,) = unpack(place, [oq0] + oq_in)
    chunk = text_chunk([texts[0]] + text_in, [gains] + others)
    rest = jnp.stack([turn(chunk, i) for i in range(1, quads)])
    across = swap(chunk, 2)
    side1 = swap(chunk, 1)
    side3 = swap(across, 1)
    ends = edges(place, ext, own, (text_in[0], text_in[-1]), near, kv_in, halos_a, qd_halos, masks, gain)
    ends_in = [swap(ends[j], j) for j in (1, 2, 3)]
    across_rest = swap(rest, 2)
    side1_rest = swap(rest, 1)
    side3_rest = swap(across_rest, 1)
    key_out, value_out = unpack(place, [ends[0]] + ends_in)
    early = text_columns(place, (0, 1), (chunk, side1), (rest, side1_rest))
    text_key_out, text_value_out, gain_out = text_columns(
        place, (2, 3), (across, side3), (across_rest, side3_rest), early
    )
    shape = queries.shape
    return (
        query_out.reshape(shape),
        key_out.reshape(shape),
        value_out.reshape(shape),
        text_key_out[None],
        text_value_out[None],
        gain_out,
    )


def solution(mesh):
    tokens = P("dp", "tm", "height", None, None)
    words = P("dp", None, None)

    return jax.shard_map(
        local,
        mesh=mesh,
        in_specs=(tokens, tokens, tokens, words, words, P(), P(), P(), P("dp"), tokens),
        out_specs=(tokens, tokens, tokens, words, words, P()),
        check_vma=False,
    )
```

time: 579 us -> 108 us (0.19)
  waiting for transfers between devices: 196 us -> 38.4 us
  local copies, waits for them, and re-layouts: 139 us -> 5.09 us
  matrix products: 95.2 us -> 0 us
  other arithmetic: 66.2 us -> 0.13 us
  blocking collectives: 41.6 us -> 0 us
  Pallas kernels: 0 us -> 20.9 us
  starting transfers between devices: 20.6 us -> 41 us
  between operations: 14.5 us -> 1.59 us
    ppermute x8 -> x30, waiting for transfers between devices: 196 us -> 38.4 us  [permute(): return lax.ppermute(x, over, pairs)]
    dot_general x72 -> x0, matrix products: 95.2 us -> none  [the longest x12 22.7 us: head_grads(): jnp.dot(weights_low.T, grad_head, preferred_element_type=jnp.float32)]
    slice x34 -> x0, local copies, waits for them, and re-layouts: 43.4 us -> none  [the longest x2 11.8 us: local(): grad_keys[:video_count]]
    psum x1 -> x0, blocking collectives: 41.6 us -> none  [local(): gain_total = lax.psum(gain_terms, ('dp', 'tm', 'height'))]
    dynamic_update_slice x36 -> x0, local copies, waits for them, and re-layouts: 29.8 us -> none  [attend_all(): lax.map(per_head, (split_heads(query_flat, head_count), split_heads(key_f...]
    and x15 -> x0, other arithmetic: 28 us -> none  [the longest x12 27.4 us: allowed_mask(): video_mask = within & key_valid[None, :]]
    pallas_call x0 -> x9, Pallas kernels: none -> 20.9 us  [call(): pl.pallas_call(kernel, grid_spec=pltpu.PrefetchScalarGridSpec(num_scalar_...]
    ppermute x8 -> x30, starting transfers between devices: 20.5 us -> 41 us  [permute(): return lax.ppermute(x, over, pairs)]
  transfers between devices with their start and end apart: 9 -> 30, of which waited for: 5 -> 14; matrix products, arithmetic and copies ran while one was open for 8% -> 0% of each run, Pallas kernels for 0% -> 8%
where the time goes in v1:
time: 108 us; the launch traced here: 107 us
  starting transfers between devices  41 us (38%)
  waiting for transfers between devices  38.4 us (36%)
  Pallas kernels  20.9 us (19%)
  local copies, waits for them, and re-layouts  5.09 us (5%)
  between operations  1.59 us (1%)
    ppermute x30, starting transfers between devices, permute(): return lax.ppermute(x, over, pairs)  41 us
    ppermute x30, waiting for transfers between devices, permute(): return lax.ppermute(x, over, pairs)  38.4 us
    pallas_call x9, Pallas kernels, call(): pl.pallas_call(kernel, grid_spec=pltpu.PrefetchScalarGridSpec(num_scalar_...  20.9 us
    unnamed x20, local copies, waits for them, and re-layouts  5.09 us
  transfers between devices with their start and end apart: 30, of which 14 were waited for; matrix products, arithmetic and copies ran while one was open for 0% of the time, Pallas kernels for 8%

profile of v1, /device:TPU:0, one launch (start us, length us, event | category | flops | bytes accessed | tf_op | source)
XLA Modules:
  0.0 107.2 jit_solution(429506374818890458)
XLA Ops:
  0.7 0.1 pad_add_fusion.place_ref
  0.8 1.1 %copy-done.2 = bf16[1,2,8,8,1536]{4,3,2,1,0:T(8,128)(2,1)S(1)} copy-done((bf16[1,2,8,8,1536]{4,3,2,1,0:T(8,128)(2,1)S(1)}, bf16[1,2,8,8,1536]{4,3,2,1,0:T(8,128)(2,1)}, u32[]{:S(2)}) %copy-start.2) | copy-done | bytes 393240
  1.8 1.0 copy-done.3
  2.8 1.0 copy-done.4
  3.8 1.0 copy-done.5
  4.8 0.9 shard_map.154
  5.8 0.6 collective-permute-start
  6.3 2.6 %collective-permute-start.1 = (bf16[2,128,384]{2,1,0:T(8,128)(2,1)S(1)}, bf16[2,128,384]{2,1,0:T(8,128)(2,1)S(1)}, u32[]{:S(2)}, u32[]{:S(2)}) collective-permute-start(bf16[2,128,384]{2,1,0:T(8,128)(2,1)S(1)} %get-tuple-element.39), channel_id=1, source_target_pairs={{0,2},{1,3},{2,0},{3,1},{4,6},{5,7},{6,4},{7,5},{8,10},{9,11},{10,... | collective-permute-start | bytes 589832 | tf_op jit(solution)/shard_map/ppermute | solution.py:436
  8.9 0.0 collective-permute-start.2
  8.9 1.7 %collective-permute-start.3 = (bf16[2,128,384]{2,1,0:T(8,128)(2,1)S(1)}, bf16[2,128,384]{2,1,0:T(8,128)(2,1)S(1)}, u32[]{:S(2)}, u32[]{:S(2)}) collective-permute-start(bf16[2,128,384]{2,1,0:T(8,128)(2,1)S(1)} %get-tuple-element.41), channel_id=1, source_target_pairs={{0,2},{1,3},{2,0},{3,1},{4,6},{5,7},{6,4},{7,5},{8,10},{9,11},{10,... | collective-permute-start | bytes 589832 | tf_op jit(solution)/shard_map/ppermute | solution.py:436
  10.6 1.3 %collective-permute-start.5 = (bf16[4,128,384]{2,1,0:T(8,128)(2,1)S(1)}, bf16[4,128,384]{2,1,0:T(8,128)(2,1)S(1)}, u32[]{:S(2)}, u32[]{:S(2)}) collective-permute-start(bf16[4,128,384]{2,1,0:T(8,128)(2,1)S(1)} %get-tuple-element.37.refs_0_.refs_3_), channel_id=1, source_target_pairs={{2,6},{3,7},{4,0},{5,1},{6,10},{7,11},{8,4},{9,5},{10,14},{11,15},... | collective-permute-start | bytes 1179656 | tf_op jit(solution)/shard_map/ppermute | solution.py:436
  11.9 0.0 collective-permute-done.refs_1_.refs_4_
  11.9 1.3 %collective-permute-start.6 = (bf16[4,128,384]{2,1,0:T(8,128)(2,1)S(1)}, bf16[4,128,384]{2,1,0:T(8,128)(2,1)S(1)}, u32[]{:S(2)}, u32[]{:S(2)}) collective-permute-start(bf16[4,128,384]{2,1,0:T(8,128)(2,1)S(1)} %collective-permute-done.refs_1_.refs_4_), channel_id=1, source_target_pairs={{2,6},{3,7},{4,0},{5,1},{6,10},{7,11},{8,4},{9,5},{10,14},{11,15},... | collective-permute-start | bytes 1179656 | tf_op jit(solution)/shard_map/ppermute | solution.py:436
  13.2 1.4 %collective-permute-done.1.refs_2_.refs_5_ = bf16[2,128,384]{2,1,0:T(8,128)(2,1)S(1)} collective-permute-done((bf16[2,128,384]{2,1,0:T(8,128)(2,1)S(1)}, bf16[2,128,384]{2,1,0:T(8,128)(2,1)S(1)}, u32[]{:S(2)}, u32[]{:S(2)}) %collective-permute-start.1) | collective-permute-done | bytes 196640 | tf_op jit(solution)/shard_map/ppermute | solution.py:436
  14.6 2.8 %collective-permute-start.4 = (bf16[2,128,384]{2,1,0:T(8,128)(2,1)S(1)}, bf16[2,128,384]{2,1,0:T(8,128)(2,1)S(1)}, u32[]{:S(2)}, u32[]{:S(2)}) collective-permute-start(bf16[2,128,384]{2,1,0:T(8,128)(2,1)S(1)} %get-tuple-element.42), channel_id=1, source_target_pairs={{0,3},{1,2},{2,1},{3,0},{4,7},{5,6},{6,5},{7,4},{8,11},{9,10},{10,... | collective-permute-start | bytes 589832 | tf_op jit(solution)/shard_map/ppermute | solution.py:436
  17.4 1.0 collective-permute-done.2.refs_3_.refs_6_
  18.4 3.5 %collective-permute-start.7 = (bf16[2,128,384]{2,1,0:T(8,128)(2,1)S(1)}, bf16[2,128,384]{2,1,0:T(8,128)(2,1)S(1)}, u32[]{:S(2)}, u32[]{:S(2)}) collective-permute-start(bf16[2,128,384]{2,1,0:T(8,128)(2,1)S(1)} %collective-permute-done.1.refs_2_.refs_5_), channel_id=1, source_target_pairs={{0,4},{1,5},{4,8},{5,9},{6,2},{7,3},{8,12},{9,13},{10,6},{11,7},{1... | collective-permute-start | bytes 589832 | tf_op jit(solution)/shard_map/ppermute | solution.py:436
  21.9 1.2 %collective-permute-done.3.refs_4_ = bf16[2,128,384]{2,1,0:T(8,128)(2,1)S(1)} collective-permute-done((bf16[2,128,384]{2,1,0:T(8,128)(2,1)S(1)}, bf16[2,128,384]{2,1,0:T(8,128)(2,1)S(1)}, u32[]{:S(2)}, u32[]{:S(2)}) %collective-permute-start.3) | collective-permute-done | bytes 196640 | tf_op jit(solution)/shard_map/ppermute | solution.py:436
  23.0 4.0 %collective-permute-start.8 = (bf16[2,128,384]{2,1,0:T(8,128)(2,1)S(1)}, bf16[2,128,384]{2,1,0:T(8,128)(2,1)S(1)}, u32[]{:S(2)}, u32[]{:S(2)}) collective-permute-start(bf16[2,128,384]{2,1,0:T(8,128)(2,1)S(1)} %collective-permute-done.2.refs_3_.refs_6_), channel_id=1, source_target_pairs={{0,4},{1,5},{4,8},{5,9},{6,2},{7,3},{8,12},{9,13},{10,6},{11,7},{1... | collective-permute-start | bytes 589832 | tf_op jit(solution)/shard_map/ppermute | solution.py:436
  27.8 0.0 copy-start.6
  27.8 1.0 copy-done.6
  28.8 0.8 shard_map.155
  29.6 1.7 %collective-permute-done.8.refs_9_ = bf16[2,128,384]{2,1,0:T(8,128)(2,1)S(1)} collective-permute-done((bf16[2,128,384]{2,1,0:T(8,128)(2,1)S(1)}, bf16[2,128,384]{2,1,0:T(8,128)(2,1)S(1)}, u32[]{:S(2)}, u32[]{:S(2)}) %collective-permute-start.8) | collective-permute-done | bytes 196640 | tf_op jit(solution)/shard_map/ppermute | solution.py:436
  31.3 0.7 collective-permute-done.6.refs_7_.refs_8_
  32.1 8.8 %shard_map.156 = (bf16[1,128,384]{2,1,0:T(8,128)(2,1)S(1)}, bf16[1,128,384]{2,1,0:T(8,128)(2,1)S(1)}, bf16[1,128,384]{2,1,0:T(8,128)(2,1)S(1)}, bf16[1,128,384]{...) custom-call(s32[3]{0:T(128)S(1)} %pad_add_fusion.place_ref, ...), custom_call_target="tpu_custom_call" | custom-call | tf_op jit(solution)/shard_map/pallas_call | solution.py:27
  40.8 1.8 %collective-permute-start.12 = (f32[136,384]{1,0:T(8,128)S(1)}, f32[136,384]{1,0:T(8,128)S(1)}, u32[]{:S(2)}, u32[]{:S(2)}) collective-permute-start(f32[136,384]{1,0:T(8,128)S(1)} %get-tuple-element.51), channel_id=1, source_target_pairs={{0,4},{1,5},{2,6},{3,7},{4,8},{5,9},{6,10},{7,11},{8,12},{9,13},{1... | collective-permute-start | bytes 626696 | tf_op jit(solution)/shard_map/ppermute | solution.py:436
  42.7 2.0 %collective-permute-start.13 = (f32[136,384]{1,0:T(8,128)S(1)}, f32[136,384]{1,0:T(8,128)S(1)}, u32[]{:S(2)}, u32[]{:S(2)}) collective-permute-start(f32[136,384]{1,0:T(8,128)S(1)} %get-tuple-element.52), channel_id=1, source_target_pairs={{0,12},{1,13},{2,14},{3,15},{4,0},{5,1},{6,2},{7,3},{8,4},{9,5},{1... | collective-permute-start | bytes 626696 | tf_op jit(solution)/shard_map/ppermute | solution.py:436
  44.7 1.0 collective-permute-start.19
  45.7 1.5 %collective-permute-start.20 = (f32[2,128]{1,0:T(2,128)S(1)}, f32[2,128]{1,0:T(2,128)S(1)}, u32[]{:S(2)}, u32[]{:S(2)}) collective-permute-start(f32[2,128]{1,0:T(2,128)S(1)} %get-tuple-element.61.refs_4_), channel_id=1, source_target_pairs={{0,16},{16,0},{1,17},{17,1},{2,18},{18,2},{3,19},{19,3},{4,20},{20... | collective-permute-start | bytes 3080 | tf_op jit(solution)/shard_map/ppermute | solution.py:436
  47.2 2.1 %collective-permute-done.20.refs_5_ = f32[2,128]{1,0:T(2,128)S(1)} collective-permute-done((f32[2,128]{1,0:T(2,128)S(1)}, f32[2,128]{1,0:T(2,128)S(1)}, u32[]{:S(2)}, u32[]{:S(2)}) %collective-permute-start.20) | collective-permute-done | bytes 1056 | tf_op jit(solution)/shard_map/ppermute | solution.py:436
  49.3 1.5 %collective-permute-done.12.refs_1_ = f32[136,384]{1,0:T(8,128)S(1)} collective-permute-done((f32[136,384]{1,0:T(8,128)S(1)}, f32[136,384]{1,0:T(8,128)S(1)}, u32[]{:S(2)}, u32[]{:S(2)}) %collective-permute-start.12) | collective-permute-done | bytes 208928 | tf_op jit(solution)/shard_map/ppermute | solution.py:436
  50.8 2.3 %collective-permute-done.13.refs_2_.refs_3_ = f32[136,384]{1,0:T(8,128)S(1)} collective-permute-done((f32[136,384]{1,0:T(8,128)S(1)}, f32[136,384]{1,0:T(8,128)S(1)}, u32[]{:S(2)}, u32[]{:S(2)}) %collective-permute-start.13) | collective-permute-done | bytes 208928 | tf_op jit(solution)/shard_map/ppermute | solution.py:436
  53.1 9.3 %collective-permute-done.19.refs_2_ = f32[136,384]{1,0:T(8,128)S(1)} collective-permute-done((f32[136,384]{1,0:T(8,128)S(1)}, f32[136,384]{1,0:T(8,128)S(1)}, u32[]{:S(2)}, u32[]{:S(2)}) %collective-permute-start.19) | collective-permute-done | bytes 208928 | tf_op jit(solution)/shard_map/ppermute | solution.py:436
  62.4 0.1 shard_map.160.refs_0_
  62.5 1.9 %collective-permute-start.25 = (bf16[136,384]{1,0:T(8,128)(2,1)S(1)}, bf16[136,384]{1,0:T(8,128)(2,1)S(1)}, u32[]{:S(2)}, u32[]{:S(2)}) collective-permute-start(bf16[136,384]{1,0:T(8,128)(2,1)S(1)} %shard_map.160.refs_0_), channel_id=1, source_target_pairs={{0,12},{1,13},{2,14},{3,15},{4,0},{5,1},{6,2},{7,3},{8,4},{9,5},{1... | collective-permute-start | bytes 313352 | tf_op jit(solution)/shard_map/ppermute | solution.py:436
  64.3 0.0 collective-permute-start.24
  64.3 0.6 collective-permute-start.23
  65.0 3.5 %collective-permute-done.25 = bf16[136,384]{1,0:T(8,128)(2,1)S(1)} collective-permute-done((bf16[136,384]{1,0:T(8,128)(2,1)S(1)}, bf16[136,384]{1,0:T(8,128)(2,1)S(1)}, u32[]{:S(2)}, u32[]{:S(2)}) %collective-permute-start.25) | collective-permute-done | bytes 104480 | tf_op jit(solution)/shard_map/ppermute | solution.py:436
  68.5 4.4 %collective-permute-done.24 = bf16[136,384]{1,0:T(8,128)(2,1)S(1)} collective-permute-done((bf16[136,384]{1,0:T(8,128)(2,1)S(1)}, bf16[136,384]{1,0:T(8,128)(2,1)S(1)}, u32[]{:S(2)}, u32[]{:S(2)}) %collective-permute-start.24) | collective-permute-done | bytes 104480 | tf_op jit(solution)/shard_map/ppermute | solution.py:436
  72.9 0.0 collective-permute-done.23
  72.9 0.1 pad_maximum_fusion.refs_2_
  72.9 1.5 %collective-permute-start.26 = (bf16[3,136,384]{2,1,0:T(8,128)(2,1)S(1)}, bf16[3,136,384]{2,1,0:T(8,128)(2,1)S(1)}, u32[]{:S(2)}, u32[]{:S(2)}) collective-permute-start(bf16[3,136,384]{2,1,0:T(8,128)(2,1)S(1)} %pad_maximum_fusion.refs_2_), channel_id=1, source_target_pairs={{0,2},{1,3},{2,0},{3,1},{4,6},{5,7},{6,4},{7,5},{8,10},{9,11},{10,... | collective-permute-start | bytes 940040 | tf_op jit(solution)/shard_map/ppermute | solution.py:436
  74.4 2.5 %collective-permute-start.14 = (bf16[2,128,384]{2,1,0:T(8,128)(2,1)S(1)}, bf16[2,128,384]{2,1,0:T(8,128)(2,1)S(1)}, u32[]{:S(2)}, u32[]{:S(2)}) collective-permute-start(bf16[2,128,384]{2,1,0:T(8,128)(2,1)S(1)} %collective-permute-done.3.refs_4_), channel_id=1, source_target_pairs={{0,4},{1,5},{4,8},{5,9},{6,2},{7,3},{8,12},{9,13},{10,6},{11,7},{1... | collective-permute-start | bytes 589832 | tf_op jit(solution)/shard_map/ppermute | solution.py:436
  76.9 4.4 %collective-permute-start.15 = (bf16[2,128,384]{2,1,0:T(8,128)(2,1)S(1)}, bf16[2,128,384]{2,1,0:T(8,128)(2,1)S(1)}, u32[]{:S(2)}, u32[]{:S(2)}) collective-permute-start(bf16[2,128,384]{2,1,0:T(8,128)(2,1)S(1)} %collective-permute-done.4.refs_5_), channel_id=1, source_target_pairs={{0,4},{1,5},{4,8},{5,9},{6,2},{7,3},{8,12},{9,13},{10,6},{11,7},{1... | collective-permute-start | bytes 589832 | tf_op jit(solution)/shard_map/ppermute | solution.py:436
  81.3 0.1 collective-permute-start.9
  81.4 0.1 collective-permute-start.10
  81.4 0.0 collective-permute-done.14.refs_9_
  81.4 1.8 %collective-permute-start.11 = (bf16[1,128,384]{2,1,0:T(8,128)(2,1)S(1)}, bf16[1,128,384]{2,1,0:T(8,128)(2,1)S(1)}, u32[]{:S(2)}, u32[]{:S(2)}) collective-permute-start(bf16[1,128,384]{2,1,0:T(8,128)(2,1)S(1)} %get-tuple-element.49), channel_id=1, source_target_pairs={{0,3},{1,2},{2,1},{3,0},{4,7},{5,6},{6,5},{7,4},{8,11},{9,10},{10,... | collective-permute-start | bytes 294920 | tf_op jit(solution)/shard_map/ppermute | solution.py:436
  83.2 1.9 %collective-permute-done.15.refs_10_ = bf16[2,128,384]{2,1,0:T(8,128)(2,1)S(1)} collective-permute-done((bf16[2,128,384]{2,1,0:T(8,128)(2,1)S(1)}, bf16[2,128,384]{2,1,0:T(8,128)(2,1)S(1)}, u32[]{:S(2)}, u32[]{:S(2)}) %collective-permute-start.15) | collective-permute-done | bytes 196640 | tf_op jit(solution)/shard_map/ppermute | solution.py:436
  85.1 0.5 collective-permute-start.27
  85.6 1.4 %collective-permute-start.21 = (bf16[136,384]{1,0:T(8,128)(2,1)S(1)}, bf16[136,384]{1,0:T(8,128)(2,1)S(1)}, u32[]{:S(2)}, u32[]{:S(2)}) collective-permute-start(bf16[136,384]{1,0:T(8,128)(2,1)S(1)} %shard_map.160.refs_0_), channel_id=1, source_target_pairs={{0,2},{1,3},{2,0},{3,1},{4,6},{5,7},{6,4},{7,5},{8,10},{9,11},{10,... | collective-permute-start | bytes 313352 | tf_op jit(solution)/shard_map/ppermute | solution.py:436
  87.0 3.5 %shard_map.158 = (bf16[2,128,384]{2,1,0:T(8,128)(2,1)S(1)}, bf16[2,128,384]{2,1,0:T(8,128)(2,1)S(1)}, bf16[2,128,384]{2,1,0:T(8,128)(2,1)S(1)}, bf16[2,128,384]{2,1,0:T(8,128)(2,1)S(1)}) custom-call(s32[3]{0:T(128)S(1)} %pad_add_fusion.place_ref, s32[3,12]{1,0:T(4,128)S(1)} %bitcast.26, f32[2,512,384]{2,1,0:T(8,128)S(1)} %get-tuple-element.50.refs_0_, ...), custom_call_target="tpu_custom_call" | custom-call | tf_op jit(solution)/shard_map/pallas_call | solution.py:27
  90.5 0.1 collective-permute-start.16
  90.6 0.0 collective-permute-done.11.refs_3_
  90.6 0.7 collective-permute-start.17
  91.3 0.0 collective-permute-done.21.refs_0_
  91.3 1.1 %collective-permute-start.18 = (bf16[2,128,384]{2,1,0:T(8,128)(2,1)S(1)}, bf16[2,128,384]{2,1,0:T(8,128)(2,1)S(1)}, u32[]{:S(2)}, u32[]{:S(2)}) collective-permute-start(bf16[2,128,384]{2,1,0:T(8,128)(2,1)S(1)} %get-tuple-element.56), channel_id=1, source_target_pairs={{0,3},{1,2},{2,1},{3,0},{4,7},{5,6},{6,5},{7,4},{8,11},{9,10},{10,... | collective-permute-start | bytes 589832 | tf_op jit(solution)/shard_map/ppermute | solution.py:436
  92.4 0.4 collective-permute-start.28
  92.8 5.6 %collective-permute-done.17.refs_2_ = bf16[2,128,384]{2,1,0:T(8,128)(2,1)S(1)} collective-permute-done((bf16[2,128,384]{2,1,0:T(8,128)(2,1)S(1)}, bf16[2,128,384]{2,1,0:T(8,128)(2,1)S(1)}, u32[]{:S(2)}, u32[]{:S(2)}) %collective-permute-start.17) | collective-permute-done | bytes 196640 | tf_op jit(solution)/shard_map/ppermute | solution.py:436
  98.4 1.3 %shard_map.157 = bf16[128,1536]{1,0:T(8,128)(2,1)} custom-call(s32[3]{0:T(128)S(1)} %pad_add_fusion.place_ref, bf16[1,128,384]{2,1,0:T(8,128)(2,1)S(1)} %get-tuple-element.46.refs_0_, bf16[1,128,384]{2,1,0:T(8,128)(2,1)S(1)} %collective-permute-done.9.refs_1_, bf16[1,128,384]{2,1,0:T(8,128)(2,1)S(1)} %collective-permute-done.10.refs_2_, ...), custom_call_target="tpu_custom_call" | custom-call | tf_op jit(solution)/shard_map/pallas_call | solution.py:27
  99.8 1.8 %collective-permute-done.18.refs_3_ = bf16[2,128,384]{2,1,0:T(8,128)(2,1)S(1)} collective-permute-done((bf16[2,128,384]{2,1,0:T(8,128)(2,1)S(1)}, bf16[2,128,384]{2,1,0:T(8,128)(2,1)S(1)}, u32[]{:S(2)}, u32[]{:S(2)}) %collective-permute-start.18) | collective-permute-done | bytes 196640 | tf_op jit(solution)/shard_map/ppermute | solution.py:436
  101.6 1.5 %shard_map.159 = (bf16[128,1536]{1,0:T(8,128)(2,1)}, bf16[128,1536]{1,0:T(8,128)(2,1)}) custom-call(s32[3]{0:T(128)S(1)} %pad_add_fusion.place_ref, bf16[2,128,384]{2,1,0:T(8,128)(2,1)S(1)} %get-tuple-element.53.refs_0_, bf16[2,128,384]{2,1,0:T(8,128)(2,1)S(1)} %collective-permute-done.16.refs_1_, bf16[2,128,384]{2,1,0:T(8,128)(2,1)S(1)} %collective-permute-done.17.refs_2_, ...), custom_call_target="tpu_custom_call" | custom-call | tf_op jit(solution)/shard_map/pallas_call | solution.py:27
  103.1 1.8 %shard_map.161 = (f32[256,1536]{1,0:T(8,128)}, f32[256,1536]{1,0:T(8,128)}, f32[2,128]{1,0:T(2,128)S(1)}) custom-call(s32[3]{0:T(128)S(1)} %pad_add_fusion.place_ref, bf16[136,384]{1,0:T(8,128)(2,1)S(1)} %shard_map.160.refs_0_, bf16[136,384]{1,0:T(8,128)(2,1)S(1)} %collective-permute-done.28.refs_1_, bf16[3,136,384]{2,1,0:T(8,128)(2,1)S(1)} %pad_maximum_fusion.refs_2_, ...), custom_call_target="tpu_custom_call" | custom-call | tf_op jit(solution)/shard_map/pallas_call | solution.py:27
  104.9 2.3 %shard_map.162 = (f32[256,1536]{1,0:T(8,128)}, f32[256,1536]{1,0:T(8,128)}, f32[2,128]{1,0:T(2,128)}) custom-call(s32[3]{0:T(128)S(1)} %pad_add_fusion.place_ref, bf16[136,384]{1,0:T(8,128)(2,1)S(1)} %collective-permute-done.21.refs_0_, bf16[136,384]{1,0:T(8,128)(2,1)S(1)} %collective-permute-done.22.refs_1_, ...), custom_call_target="tpu_custom_call", output_to_operand_aliasing={{0}: (6, {}), {1}: (7, {})} | custom-call | tf_op jit(solution)/shard_map/pallas_call | solution.py:27
  (27 shorter events, 0.1 us)
Async XLA Ops:
  0.6 27.1 %copy-start.1 = (bf16[1,256,1536]{2,1,0:T(8,128)(2,1)S(1)}, bf16[1,256,1536]{2,1,0:T(8,128)(2,1)}, u32[]{:S(2)}) copy-start(bf16[1,256,1536]{2,1,0:T(8,128)(2,1)} %param.15) | copy-start | bytes 2359300
  0.6 27.1 %copy-start = (bf16[1,256,1536]{2,1,0:T(8,128)(2,1)S(1)}, bf16[1,256,1536]{2,1,0:T(8,128)(2,1)}, u32[]{:S(2)}) copy-start(bf16[1,256,1536]{2,1,0:T(8,128)(2,1)} %param.14) | copy-start | bytes 2359300
  0.7 1.1 %copy-start.2 = (bf16[1,2,8,8,1536]{4,3,2,1,0:T(8,128)(2,1)S(1)}, bf16[1,2,8,8,1536]{4,3,2,1,0:T(8,128)(2,1)}, u32[]{:S(2)}) copy-start(bf16[1,2,8,8,1536]{4,3,2,1,0:T(8,128)(2,1)} %param.12) | copy-start | bytes 1179652
  1.8 1.0 copy-start.3
  2.8 1.0 copy-start.4
  3.8 1.0 copy-start.5
  4.8 22.9 %copy-start.8 = (f32[128]{0:T(128)S(1)}, f32[128]{0:T(128)}, u32[]{:S(2)}) copy-start(f32[128]{0:T(128)} %param.16) | copy-start | bytes 1540
  4.8 22.9 %copy-start.9 = (f32[128]{0:T(128)S(1)}, f32[128]{0:T(128)}, u32[]{:S(2)}) copy-start(f32[128]{0:T(128)} %param.17) | copy-start | bytes 1540
  4.8 27.2 %copy-start.7 = (s32[12,3]{0,1:T(4,128)S(1)}, s32[12,3]{0,1:T(4,128)}, u32[]{:S(2)}) copy-start(s32[12,3]{0,1:T(4,128)} %param.18) | copy-start | bytes 436
  5.8 6.2 %collective-permute-start = (bf16[4,128,384]{2,1,0:T(8,128)(2,1)S(1)}, bf16[4,128,384]{2,1,0:T(8,128)(2,1)S(1)}, u32[]{:S(2)}, u32[]{:S(2)}) collective-permute-start(bf16[4,128,384]{2,1,0:T(8,128)(2,1)S(1)} %get-tuple-element.38), channel_id=1, source_target_pairs={{0,1},{1,0},{2,3},{3,2},{4,5},{5,4},{6,7},{7,6},{8,9},{9,8},{10,11... | collective-permute-start | bytes 1179656 | tf_op jit(solution)/shard_map/ppermute | solution.py:436
  6.3 8.3 %collective-permute-start.1 = (bf16[2,128,384]{2,1,0:T(8,128)(2,1)S(1)}, bf16[2,128,384]{2,1,0:T(8,128)(2,1)S(1)}, u32[]{:S(2)}, u32[]{:S(2)}) collective-permute-start(bf16[2,128,384]{2,1,0:T(8,128)(2,1)S(1)} %get-tuple-element.39), channel_id=1, source_target_pairs={{0,2},{1,3},{2,0},{3,1},{4,6},{5,7},{6,4},{7,5},{8,10},{9,11},{10,... | collective-permute-start | bytes 589832 | tf_op jit(solution)/shard_map/ppermute | solution.py:436
  8.9 9.5 %collective-permute-start.2 = (bf16[2,128,384]{2,1,0:T(8,128)(2,1)S(1)}, bf16[2,128,384]{2,1,0:T(8,128)(2,1)S(1)}, u32[]{:S(2)}, u32[]{:S(2)}) collective-permute-start(bf16[2,128,384]{2,1,0:T(8,128)(2,1)S(1)} %get-tuple-element.40), channel_id=1, source_target_pairs={{0,3},{1,2},{2,1},{3,0},{4,7},{5,6},{6,5},{7,4},{8,11},{9,10},{10,... | collective-permute-start | bytes 589832 | tf_op jit(solution)/shard_map/ppermute | solution.py:436
  8.9 14.1 %collective-permute-start.3 = (bf16[2,128,384]{2,1,0:T(8,128)(2,1)S(1)}, bf16[2,128,384]{2,1,0:T(8,128)(2,1)S(1)}, u32[]{:S(2)}, u32[]{:S(2)}) collective-permute-start(bf16[2,128,384]{2,1,0:T(8,128)(2,1)S(1)} %get-tuple-element.41), channel_id=1, source_target_pairs={{0,2},{1,3},{2,0},{3,1},{4,6},{5,7},{6,4},{7,5},{8,10},{9,11},{10,... | collective-permute-start | bytes 589832 | tf_op jit(solution)/shard_map/ppermute | solution.py:436
  10.6 20.7 %collective-permute-start.5 = (bf16[4,128,384]{2,1,0:T(8,128)(2,1)S(1)}, bf16[4,128,384]{2,1,0:T(8,128)(2,1)S(1)}, u32[]{:S(2)}, u32[]{:S(2)}) collective-permute-start(bf16[4,128,384]{2,1,0:T(8,128)(2,1)S(1)} %get-tuple-element.37.refs_0_.refs_3_), channel_id=1, source_target_pairs={{2,6},{3,7},{4,0},{5,1},{6,10},{7,11},{8,4},{9,5},{10,14},{11,15},... | collective-permute-start | bytes 1179656 | tf_op jit(solution)/shard_map/ppermute | solution.py:436
  11.9 20.1 %collective-permute-start.6 = (bf16[4,128,384]{2,1,0:T(8,128)(2,1)S(1)}, bf16[4,128,384]{2,1,0:T(8,128)(2,1)S(1)}, u32[]{:S(2)}, u32[]{:S(2)}) collective-permute-start(bf16[4,128,384]{2,1,0:T(8,128)(2,1)S(1)} %collective-permute-done.refs_1_.refs_4_), channel_id=1, source_target_pairs={{2,6},{3,7},{4,0},{5,1},{6,10},{7,11},{8,4},{9,5},{10,14},{11,15},... | collective-permute-start | bytes 1179656 | tf_op jit(solution)/shard_map/ppermute | solution.py:436
  14.6 15.0 %collective-permute-start.4 = (bf16[2,128,384]{2,1,0:T(8,128)(2,1)S(1)}, bf16[2,128,384]{2,1,0:T(8,128)(2,1)S(1)}, u32[]{:S(2)}, u32[]{:S(2)}) collective-permute-start(bf16[2,128,384]{2,1,0:T(8,128)(2,1)S(1)} %get-tuple-element.42), channel_id=1, source_target_pairs={{0,3},{1,2},{2,1},{3,0},{4,7},{5,6},{6,5},{7,4},{8,11},{9,10},{10,... | collective-permute-start | bytes 589832 | tf_op jit(solution)/shard_map/ppermute | solution.py:436
  18.4 11.2 %collective-permute-start.7 = (bf16[2,128,384]{2,1,0:T(8,128)(2,1)S(1)}, bf16[2,128,384]{2,1,0:T(8,128)(2,1)S(1)}, u32[]{:S(2)}, u32[]{:S(2)}) collective-permute-start(bf16[2,128,384]{2,1,0:T(8,128)(2,1)S(1)} %collective-permute-done.1.refs_2_.refs_5_), channel_id=1, source_target_pairs={{0,4},{1,5},{4,8},{5,9},{6,2},{7,3},{8,12},{9,13},{10,6},{11,7},{1... | collective-permute-start | bytes 589832 | tf_op jit(solution)/shard_map/ppermute | solution.py:436
  23.0 8.3 %collective-permute-start.8 = (bf16[2,128,384]{2,1,0:T(8,128)(2,1)S(1)}, bf16[2,128,384]{2,1,0:T(8,128)(2,1)S(1)}, u32[]{:S(2)}, u32[]{:S(2)}) collective-permute-start(bf16[2,128,384]{2,1,0:T(8,128)(2,1)S(1)} %collective-permute-done.2.refs_3_.refs_6_), channel_id=1, source_target_pairs={{0,4},{1,5},{4,8},{5,9},{6,2},{7,3},{8,12},{9,13},{10,6},{11,7},{1... | collective-permute-start | bytes 589832 | tf_op jit(solution)/shard_map/ppermute | solution.py:436
  27.8 1.0 copy-start.6
  40.8 9.9 %collective-permute-start.12 = (f32[136,384]{1,0:T(8,128)S(1)}, f32[136,384]{1,0:T(8,128)S(1)}, u32[]{:S(2)}, u32[]{:S(2)}) collective-permute-start(f32[136,384]{1,0:T(8,128)S(1)} %get-tuple-element.51), channel_id=1, source_target_pairs={{0,4},{1,5},{2,6},{3,7},{4,8},{5,9},{6,10},{7,11},{8,12},{9,13},{1... | collective-permute-start | bytes 626696 | tf_op jit(solution)/shard_map/ppermute | solution.py:436
  42.7 10.4 %collective-permute-start.13 = (f32[136,384]{1,0:T(8,128)S(1)}, f32[136,384]{1,0:T(8,128)S(1)}, u32[]{:S(2)}, u32[]{:S(2)}) collective-permute-start(f32[136,384]{1,0:T(8,128)S(1)} %get-tuple-element.52), channel_id=1, source_target_pairs={{0,12},{1,13},{2,14},{3,15},{4,0},{5,1},{6,2},{7,3},{8,4},{9,5},{1... | collective-permute-start | bytes 626696 | tf_op jit(solution)/shard_map/ppermute | solution.py:436
  44.7 17.7 %collective-permute-start.19 = (f32[136,384]{1,0:T(8,128)S(1)}, f32[136,384]{1,0:T(8,128)S(1)}, u32[]{:S(2)}, u32[]{:S(2)}) collective-permute-start(f32[136,384]{1,0:T(8,128)S(1)} %get-tuple-element.60), channel_id=1, source_target_pairs={{0,8},{1,9},{2,10},{3,11},{4,12},{5,13},{6,14},{7,15},{8,0},{9,1},... | collective-permute-start | bytes 626696 | tf_op jit(solution)/shard_map/ppermute | solution.py:436
  45.7 3.6 %collective-permute-start.20 = (f32[2,128]{1,0:T(2,128)S(1)}, f32[2,128]{1,0:T(2,128)S(1)}, u32[]{:S(2)}, u32[]{:S(2)}) collective-permute-start(f32[2,128]{1,0:T(2,128)S(1)} %get-tuple-element.61.refs_4_), channel_id=1, source_target_pairs={{0,16},{16,0},{1,17},{17,1},{2,18},{18,2},{3,19},{19,3},{4,20},{20... | collective-permute-start | bytes 3080 | tf_op jit(solution)/shard_map/ppermute | solution.py:436
  62.5 6.0 %collective-permute-start.25 = (bf16[136,384]{1,0:T(8,128)(2,1)S(1)}, bf16[136,384]{1,0:T(8,128)(2,1)S(1)}, u32[]{:S(2)}, u32[]{:S(2)}) collective-permute-start(bf16[136,384]{1,0:T(8,128)(2,1)S(1)} %shard_map.160.refs_0_), channel_id=1, source_target_pairs={{0,12},{1,13},{2,14},{3,15},{4,0},{5,1},{6,2},{7,3},{8,4},{9,5},{1... | collective-permute-start | bytes 313352 | tf_op jit(solution)/shard_map/ppermute | solution.py:436
  64.3 8.5 %collective-permute-start.24 = (bf16[136,384]{1,0:T(8,128)(2,1)S(1)}, bf16[136,384]{1,0:T(8,128)(2,1)S(1)}, u32[]{:S(2)}, u32[]{:S(2)}) collective-permute-start(bf16[136,384]{1,0:T(8,128)(2,1)S(1)} %shard_map.160.refs_0_), channel_id=1, source_target_pairs={{0,8},{1,9},{2,10},{3,11},{4,12},{5,13},{6,14},{7,15},{8,0},{9,1},... | collective-permute-start | bytes 313352 | tf_op jit(solution)/shard_map/ppermute | solution.py:436
  64.3 8.5 %collective-permute-start.23 = (bf16[136,384]{1,0:T(8,128)(2,1)S(1)}, bf16[136,384]{1,0:T(8,128)(2,1)S(1)}, u32[]{:S(2)}, u32[]{:S(2)}) collective-permute-start(bf16[136,384]{1,0:T(8,128)(2,1)S(1)} %shard_map.160.refs_0_), channel_id=1, source_target_pairs={{0,4},{1,5},{2,6},{3,7},{4,8},{5,9},{6,10},{7,11},{8,12},{9,13},{1... | collective-permute-start | bytes 313352 | tf_op jit(solution)/shard_map/ppermute | solution.py:436
  72.9 12.2 %collective-permute-start.26 = (bf16[3,136,384]{2,1,0:T(8,128)(2,1)S(1)}, bf16[3,136,384]{2,1,0:T(8,128)(2,1)S(1)}, u32[]{:S(2)}, u32[]{:S(2)}) collective-permute-start(bf16[3,136,384]{2,1,0:T(8,128)(2,1)S(1)} %pad_maximum_fusion.refs_2_), channel_id=1, source_target_pairs={{0,2},{1,3},{2,0},{3,1},{4,6},{5,7},{6,4},{7,5},{8,10},{9,11},{10,... | collective-permute-start | bytes 940040 | tf_op jit(solution)/shard_map/ppermute | solution.py:436
  74.4 7.0 %collective-permute-start.14 = (bf16[2,128,384]{2,1,0:T(8,128)(2,1)S(1)}, bf16[2,128,384]{2,1,0:T(8,128)(2,1)S(1)}, u32[]{:S(2)}, u32[]{:S(2)}) collective-permute-start(bf16[2,128,384]{2,1,0:T(8,128)(2,1)S(1)} %collective-permute-done.3.refs_4_), channel_id=1, source_target_pairs={{0,4},{1,5},{4,8},{5,9},{6,2},{7,3},{8,12},{9,13},{10,6},{11,7},{1... | collective-permute-start | bytes 589832 | tf_op jit(solution)/shard_map/ppermute | solution.py:436
  76.9 8.2 %collective-permute-start.15 = (bf16[2,128,384]{2,1,0:T(8,128)(2,1)S(1)}, bf16[2,128,384]{2,1,0:T(8,128)(2,1)S(1)}, u32[]{:S(2)}, u32[]{:S(2)}) collective-permute-start(bf16[2,128,384]{2,1,0:T(8,128)(2,1)S(1)} %collective-permute-done.4.refs_5_), channel_id=1, source_target_pairs={{0,4},{1,5},{4,8},{5,9},{6,2},{7,3},{8,12},{9,13},{10,6},{11,7},{1... | collective-permute-start | bytes 589832 | tf_op jit(solution)/shard_map/ppermute | solution.py:436
  81.3 4.4 %collective-permute-start.9 = (bf16[1,128,384]{2,1,0:T(8,128)(2,1)S(1)}, bf16[1,128,384]{2,1,0:T(8,128)(2,1)S(1)}, u32[]{:S(2)}, u32[]{:S(2)}) collective-permute-start(bf16[1,128,384]{2,1,0:T(8,128)(2,1)S(1)} %get-tuple-element.47), channel_id=1, source_target_pairs={{0,1},{1,0},{2,3},{3,2},{4,5},{5,4},{6,7},{7,6},{8,9},{9,8},{10,11... | collective-permute-start | bytes 294920 | tf_op jit(solution)/shard_map/ppermute | solution.py:436
  81.4 9.1 %collective-permute-start.10 = (bf16[1,128,384]{2,1,0:T(8,128)(2,1)S(1)}, bf16[1,128,384]{2,1,0:T(8,128)(2,1)S(1)}, u32[]{:S(2)}, u32[]{:S(2)}) collective-permute-start(bf16[1,128,384]{2,1,0:T(8,128)(2,1)S(1)} %get-tuple-element.48), channel_id=1, source_target_pairs={{0,2},{1,3},{2,0},{3,1},{4,6},{5,7},{6,4},{7,5},{8,10},{9,11},{10,... | collective-permute-start | bytes 294920 | tf_op jit(solution)/shard_map/ppermute | solution.py:436
  81.4 9.1 %collective-permute-start.11 = (bf16[1,128,384]{2,1,0:T(8,128)(2,1)S(1)}, bf16[1,128,384]{2,1,0:T(8,128)(2,1)S(1)}, u32[]{:S(2)}, u32[]{:S(2)}) collective-permute-start(bf16[1,128,384]{2,1,0:T(8,128)(2,1)S(1)} %get-tuple-element.49), channel_id=1, source_target_pairs={{0,3},{1,2},{2,1},{3,0},{4,7},{5,6},{6,5},{7,4},{8,11},{9,10},{10,... | collective-permute-start | bytes 294920 | tf_op jit(solution)/shard_map/ppermute | solution.py:436
  85.1 17.9 %collective-permute-start.29 = (bf16[3,136,384]{2,1,0:T(8,128)(2,1)S(1)}, bf16[3,136,384]{2,1,0:T(8,128)(2,1)S(1)}, u32[]{:S(2)}, u32[]{:S(2)}) collective-permute-start(bf16[3,136,384]{2,1,0:T(8,128)(2,1)S(1)} %pad_maximum_fusion.refs_2_), channel_id=1, source_target_pairs={{0,1},{1,0},{2,3},{3,2},{4,5},{5,4},{6,7},{7,6},{8,9},{9,8},{10,11... | collective-permute-start | bytes 940040 | tf_op jit(solution)/shard_map/ppermute | solution.py:436
  85.1 19.7 %collective-permute-start.27 = (bf16[3,136,384]{2,1,0:T(8,128)(2,1)S(1)}, bf16[3,136,384]{2,1,0:T(8,128)(2,1)S(1)}, u32[]{:S(2)}, u32[]{:S(2)}) collective-permute-start(bf16[3,136,384]{2,1,0:T(8,128)(2,1)S(1)} %collective-permute-done.26.refs_2_), channel_id=1, source_target_pairs={{0,1},{1,0},{2,3},{3,2},{4,5},{5,4},{6,7},{7,6},{8,9},{9,8},{10,11... | collective-permute-start | bytes 940040 | tf_op jit(solution)/shard_map/ppermute | solution.py:436
  85.6 5.7 %collective-permute-start.21 = (bf16[136,384]{1,0:T(8,128)(2,1)S(1)}, bf16[136,384]{1,0:T(8,128)(2,1)S(1)}, u32[]{:S(2)}, u32[]{:S(2)}) collective-permute-start(bf16[136,384]{1,0:T(8,128)(2,1)S(1)} %shard_map.160.refs_0_), channel_id=1, source_target_pairs={{0,2},{1,3},{2,0},{3,1},{4,6},{5,7},{6,4},{7,5},{8,10},{9,11},{10,... | collective-permute-start | bytes 313352 | tf_op jit(solution)/shard_map/ppermute | solution.py:436
  90.5 1.9 %collective-permute-start.16 = (bf16[2,128,384]{2,1,0:T(8,128)(2,1)S(1)}, bf16[2,128,384]{2,1,0:T(8,128)(2,1)S(1)}, u32[]{:S(2)}, u32[]{:S(2)}) collective-permute-start(bf16[2,128,384]{2,1,0:T(8,128)(2,1)S(1)} %get-tuple-element.54), channel_id=1, source_target_pairs={{0,1},{1,0},{2,3},{3,2},{4,5},{5,4},{6,7},{7,6},{8,9},{9,8},{10,11... | collective-permute-start | bytes 589832 | tf_op jit(solution)/shard_map/ppermute | solution.py:436
  90.6 7.8 %collective-permute-start.17 = (bf16[2,128,384]{2,1,0:T(8,128)(2,1)S(1)}, bf16[2,128,384]{2,1,0:T(8,128)(2,1)S(1)}, u32[]{:S(2)}, u32[]{:S(2)}) collective-permute-start(bf16[2,128,384]{2,1,0:T(8,128)(2,1)S(1)} %get-tuple-element.55), channel_id=1, source_target_pairs={{0,2},{1,3},{2,0},{3,1},{4,6},{5,7},{6,4},{7,5},{8,10},{9,11},{10,... | collective-permute-start | bytes 589832 | tf_op jit(solution)/shard_map/ppermute | solution.py:436
  91.3 10.2 %collective-permute-start.18 = (bf16[2,128,384]{2,1,0:T(8,128)(2,1)S(1)}, bf16[2,128,384]{2,1,0:T(8,128)(2,1)S(1)}, u32[]{:S(2)}, u32[]{:S(2)}) collective-permute-start(bf16[2,128,384]{2,1,0:T(8,128)(2,1)S(1)} %get-tuple-element.56), channel_id=1, source_target_pairs={{0,3},{1,2},{2,1},{3,0},{4,7},{5,6},{6,5},{7,4},{8,11},{9,10},{10,... | collective-permute-start | bytes 589832 | tf_op jit(solution)/shard_map/ppermute | solution.py:436
  92.4 10.6 %collective-permute-start.28 = (bf16[136,384]{1,0:T(8,128)(2,1)S(1)}, bf16[136,384]{1,0:T(8,128)(2,1)S(1)}, u32[]{:S(2)}, u32[]{:S(2)}) collective-permute-start(bf16[136,384]{1,0:T(8,128)(2,1)S(1)} %shard_map.160.refs_0_), channel_id=1, source_target_pairs={{0,1},{1,0},{2,3},{3,2},{4,5},{5,4},{6,7},{7,6},{8,9},{9,8},{10,11... | collective-permute-start | bytes 313352 | tf_op jit(solution)/shard_map/ppermute | solution.py:436
  98.4 6.4 %collective-permute-start.22 = (bf16[136,384]{1,0:T(8,128)(2,1)S(1)}, bf16[136,384]{1,0:T(8,128)(2,1)S(1)}, u32[]{:S(2)}, u32[]{:S(2)}) collective-permute-start(bf16[136,384]{1,0:T(8,128)(2,1)S(1)} %collective-permute-done.21.refs_0_), channel_id=1, source_target_pairs={{0,1},{1,0},{2,3},{3,2},{4,5},{5,4},{6,7},{7,6},{8,9},{9,8},{10,11... | collective-permute-start | bytes 313352 | tf_op jit(solution)/shard_map/ppermute | solution.py:436

commit v2 on v1

--- a/solution.py
+++ b/solution.py
@@ -23,7 +23,8 @@
 
 def call(kernel, scalars, operands, outputs, scratch=(), aliases=None, limit=24):
     spec = {"vmem": VMEM, "hbm": HBM, "out": VMEM}
-    held = [pltpu.with_memory_space_constraint(x, pltpu.VMEM) if space == "vmem" else x for x, space in operands]
+    spaces = {"vmem": pltpu.VMEM, "hbm": pltpu.HBM}
+    held = [pltpu.with_memory_space_constraint(x, spaces[space]) for x, space in operands]
     return pl.pallas_call(
         kernel,
         grid_spec=pltpu.PrefetchScalarGridSpec(
@@ -93,6 +94,21 @@
     )
 
 
+def join(groups):
+    arrays = []
+    for group in groups:
+        arrays += [x for x, _, _ in group if all(x is not y for y in arrays)]
+    index = lambda x: [x is y for y in arrays].index(True)
+
+    def kernel(*refs):
+        for group, out in zip(groups, refs[len(arrays):]):
+            for i, (x, first, last) in enumerate(group):
+                out[i] = refs[index(x)][first:last]
+
+    outputs = [((len(group), group[0][2] - group[0][1], *group[0][0].shape[1:]), arrays[0].dtype, "vmem") for group in groups]
+    return call(kernel, [], [(x, "vmem") for x in arrays], outputs)
+
+
 def unpack(place, pieces):
     count, rows, width = pieces[0].shape
 
@@ -157,8 +173,8 @@
     scale = 128 ** -0.5
 
     def kernel(place_ref, ext_ref, len_ref, *refs):
-        n0, n1, kv2, kv3, qd2, qd3, ha0, ha1, hb0, hb1, text_ref, mask_ref, gain_ref = refs[:13]
-        oqs, own, ogain = refs[13:17], refs[17], refs[18]
+        n0, n1, kv2, kv3, qd2, qd3, ha, hb, text_ref, mask_ref, gain_ref = refs[:11]
+        oqs, own, ogain, stats = refs[11:15], refs[15], refs[16], refs[17:19]
         messages = refs[19:19 + chunks]
         kn, vs, kx, qn, grads, qx, qr, dk, dv, ends = refs[19 + chunks:]
         g, p, last = place_ref[0], place_ref[1], place_ref[2]
@@ -172,8 +188,8 @@
         word = lax.broadcasted_iota(jnp.int32, (text_count, 128), 0)
         kn[video:, 128:] = hidden(word < len_ref[0])
         ogain[...] = jnp.zeros((2, 128), F32)
-        for out in messages:
-            out[2 * chunk:, :] = jnp.zeros((8, width), F32)
+        for out in stats:
+            out[...] = jnp.zeros((8, width), F32)
 
         def one_head(h, _):
             lanes = pl.ds(pl.multiple_of(h * 128, 128), 128)
@@ -181,7 +197,7 @@
             e0, e1, e2 = ext_ref[0, head], ext_ref[1, head].astype(F32), ext_ref[2, head].astype(F32)
 
             sources = [(r, start + tile) for r, start in zip((n0, n1, kv2, kv3), own_at)]
-            sources += list(zip((ha0, ha1, hb0, hb1), halo_at))
+            sources += list(zip((ha.at[0], ha.at[1], hb.at[0], hb.at[1]), halo_at))
             for r, start in sources:
                 hat, _ = unit(r[0, :, lanes])
                 kx[at(start), :] = hat
@@ -223,11 +239,10 @@
                 attn = sum(dot(vs[x, :], w, (0, 0)) for x, w in zip(parts[t], low))
                 prob_grad = [dot(vs[x, :], grad, (1, 1)) for x in parts[t]]
                 delta = jnp.sum(grad.astype(F32).T * attn, axis=0, keepdims=True)
-                message = messages[chunks - 1] if t == 0 else messages[1]
                 for i, number in enumerate((top, share, delta)):
                     for side in range(2):
-                        row = 2 * chunk + 2 * i + side
-                        message[row:row + 1, lanes] = number[:, side * 128:side * 128 + 128]
+                        row = 2 * i + side
+                        stats[t][row:row + 1, lanes] = number[:, side * 128:side * 128 + 128]
                 score_grad = [(w * (y - delta)).astype(BF16) for w, y in zip(probs, prob_grad)]
                 dqn = sum(dot(kn[x, :128], s, (0, 0)) for x, s in zip(parts[t], score_grad)).T * scale
                 mine = slice((1 - t) * tile, (3 - t) * tile)
@@ -271,7 +286,8 @@
         kernel, [place, window_ext, text_len], [(x, "vmem") for x in operands],
         [((1, slot, width), BF16, "vmem")] * 4
         + [((2, 2 * tile, width), F32, "vmem"), ((2, 128), F32, "vmem")]
-        + [((2 * chunk + 8, width), F32, "vmem")] * chunks,
+        + [((8, width), F32, "vmem")] * 2
+        + [((2 * chunk, width), F32, "vmem")] * chunks,
         [
             pltpu.VMEM((video + text_count, 256), BF16),
             pltpu.VMEM((video + text_count, 128), BF16),
@@ -287,17 +303,16 @@
     )
 
 
-def edges(place, window_ext, own, messages, near, kv, halos_a, halos_b, masks, gain):
+def edges(place, window_ext, own, messages, near, kv, halos, masks, gain):
     _, slot, width = near[0].shape
     heads = width // 128
     tile = 2 * slot
-    chunk = (messages[0].shape[0] - 8) // 2
     scale = 128 ** -0.5
 
     def kernel(place_ref, ext_ref, *refs):
-        own_ref, before_ref, after_ref, n0, n1, kv2, kv3, ha0, ha1, hb0, hb1 = refs[:11]
-        mask_ref, gain_ref, o0, o1, o2, o3 = refs[11:17]
-        kn, vs, kx, kr, qn, grads, ends = refs[17:]
+        own_ref, before_ref, after_ref, n0, n1, kv2, kv3, ha, hb = refs[:9]
+        mask_ref, gain_ref, o0, o1, o2, o3 = refs[9:15]
+        kn, vs, kx, kr, qn, grads, ends = refs[15:]
         g, p, last = place_ref[0], place_ref[1], place_ref[2]
         gq, gk = gain_ref[0:1, :], gain_ref[1:2, :]
         at = lambda start: pl.ds(pl.multiple_of(start, slot), slot)
@@ -315,16 +330,16 @@
                 kr[at(start), :] = jnp.broadcast_to(inverse, hat.shape)
                 kn[at(start), :128] = (hat * gk).astype(BF16)
                 vs[at(start), :] = r[1, :, lanes]
-            for r, i, start in zip((ha0, ha1, hb0, hb1), (2, 2, 0, 0), halo_at):
-                qn[at(start), :128] = (unit(r[i, :, lanes])[0] * gq).astype(BF16)
-                grads[at(start), :] = r[i + 1, :, lanes]
+            for r, start in zip((ha.at[0], ha.at[1], hb.at[0], hb.at[1]), halo_at):
+                qn[at(start), :128] = (unit(r[0, :, lanes])[0] * gq).astype(BF16)
+                grads[at(start), :] = r[1, :, lanes]
             close = (mask_ref[0] <= e1) & (mask_ref[1] <= e2) & (e0 >= 1)
             for t in range(2):
                 kn[t * tile:(t + 1) * tile, 128:] = hidden(close & ((p > 0) if t == 0 else (p < last)))
             for t, message in enumerate((before_ref, after_ref)):
                 rows = slice(t * tile, (t + 1) * tile)
                 top, share, delta = [
-                    jnp.concatenate([message[2 * chunk + i:2 * chunk + i + 1, lanes] for i in (n, n + 1)], axis=1)
+                    jnp.concatenate([message[i:i + 1, lanes] for i in (n, n + 1)], axis=1)
                     for n in (0, 2, 4)
                 ]
                 query, grad = qn[rows, :], grads[rows, :]
@@ -345,7 +360,7 @@
 
         lax.fori_loop(0, heads, one_head, 0)
 
-    operands = [own, *messages, *near, *kv, *halos_a, *halos_b, masks, gain]
+    operands = [own, *messages, *near, *kv, *halos, masks, gain]
     return call(
         kernel, [place, window_ext], [(x, "vmem") for x in operands],
         [((2, slot, width), BF16, "vmem")] * 4,
@@ -362,14 +377,13 @@
 
 
 def text_chunk(parts, gains):
-    padded, width = parts[0].shape
-    rows = padded - 8
+    rows, width = parts[0].shape
 
     def kernel(*refs):
         sums, tails, out_ref = refs[:len(parts)], refs[len(parts):-1], refs[-1]
-        total = sums[0][:rows, :]
+        total = sums[0][...]
         for ref in sums[1:]:
-            total = total + ref[:rows, :]
+            total = total + ref[...]
         out_ref[:rows, :] = total.astype(BF16)
         out_ref[rows:, :] = jnp.zeros((8, width), BF16)
         rest = tails[0][...]
@@ -380,7 +394,7 @@
             out_ref[rows + 2 * i:rows + 2 * i + 2, :128] = part
             rest = rest - part.astype(F32)
 
-    return call(kernel, [], [(x, "vmem") for x in parts + gains], [((padded, width), BF16, "vmem")])[0]
+    return call(kernel, [], [(x, "vmem") for x in parts + gains], [((rows + 8, width), BF16, "vmem")])[0]
 
 
 def text_columns(place, members, firsts, rests, earlier=None):
@@ -458,14 +472,17 @@
         place, (text_keys[0], text_values[0]), (gain_q.reshape(1, -1), gain_k.reshape(1, -1)), table
     )
     near = [near0, swap(near1, 1)]
-    halos_a = [move(near[0], out_a), move(near[1], out_a)]
-    kv_halos = [move(kv_in[0], out_b), move(kv_in[1], out_b)]
-    qd_halos = [move(qd_in[0], out_b), move(qd_in[1], out_b)]
+    kv_a, qd_a = join([[(x, 0, 2) for x in near], [(x, 2, 4) for x in near]])
+    (kv_b,) = join([[(x, 0, 2) for x in kv_in]])
+    (qd_b,) = join([[(x, 0, 2) for x in qd_in]])
+    kv_halos = [move(kv_a, out_a), move(kv_b, out_b)]
+    qd_halos = [move(qd_a, out_a), move(qd_b, out_b)]
     ext = window_ext.T
 
-    oq0, oq1, oq2, oq3, own, gains, *texts = attention(
-        place, ext, text_len, near, kv_in, qd_in, halos_a + kv_halos, words, masks, space, gain, quads
-    )
+    oq0, oq1, oq2, oq3, own, gains, stats0, stats1, *texts = attention(
+        place, ext, text_len, near, kv_in, qd_in, kv_halos, words, masks, space, gain, quads
+    )
+    after, before = move(stats0, lambda a: -1), move(stats1, lambda a: 1)
     text_in = [turn(texts[i], i) for i in range(1, quads)]
     others = [permute(gains, [(n, (n + i) % samples) for n in range(samples)], "dp") for i in range(1, samples)]
     oq_in = [swap(x, j) for x, j in zip((oq1, oq2, oq3), (1, 2, 3))]
@@ -475,7 +492,7 @@
     across = swap(chunk, 2)
     side1 = swap(chunk, 1)
     side3 = swap(across, 1)
-    ends = edges(place, ext, own, (text_in[0], text_in[-1]), near, kv_in, halos_a, qd_halos, masks, gain)
+    ends = edges(place, ext, own, (before, after), near, kv_in, qd_halos, masks, gain)
     ends_in = [swap(ends[j], j) for j in (1, 2, 3)]
     across_rest = swap(rest, 2)
     side1_rest = swap(rest, 1)

time: 108 us -> 110 us (1.019)
  local copies, waits for them, and re-layouts: 5.09 us -> 0.01 us
  waiting for transfers between devices: 38.4 us -> 43.2 us
  Pallas kernels: 20.9 us -> 23.4 us
    unnamed x20 -> x2, local copies, waits for them, and re-layouts: 5.09 us -> 0.01 us
    ppermute x30, waiting for transfers between devices: 38.4 us -> 43.2 us  [permute(): return lax.ppermute(x, over, pairs)]
    pallas_call x9 -> x12, Pallas kernels: 20.9 us -> 23.4 us  [call(): pl.pallas_call(kernel, grid_spec=pltpu.PrefetchScalarGridSpec(num_scalar_...]
  transfers between devices with their start and end apart: 30 -> 30, of which waited for: 14 -> 15; matrix products, arithmetic and copies ran while one was open for 0% -> 0% of each run, Pallas kernels for 8% -> 9%
where the time goes in v2:
time: 110 us; the launch traced here: 109 us
  waiting for transfers between devices  43.2 us (39%)
  starting transfers between devices  41 us (37%)
  Pallas kernels  23.4 us (21%)
  between operations  1.52 us (1%)
    ppermute x30, waiting for transfers between devices, permute(): return lax.ppermute(x, over, pairs)  43.2 us
    ppermute x30, starting transfers between devices, permute(): return lax.ppermute(x, over, pairs)  41 us
    pallas_call x12, Pallas kernels, call(): pl.pallas_call(kernel, grid_spec=pltpu.PrefetchScalarGridSpec(num_scalar_...  23.4 us
  transfers between devices with their start and end apart: 30, of which 15 were waited for; matrix products, arithmetic and copies ran while one was open for 0% of the time, Pallas kernels for 9%

profile of v2, /device:TPU:0, one launch (start us, length us, event | category | flops | bytes accessed | tf_op | source)
XLA Modules:
  0.0 109.2 jit_solution(7534853370463128854)
XLA Ops:
  0.7 0.1 pad_add_fusion.place_ref
  0.7 2.2 %shard_map.154 = (bf16[4,128,384]{2,1,0:T(8,128)(2,1)S(1)}, bf16[4,128,384]{2,1,0:T(8,128)(2,1)S(1)}, bf16[2,128,384]{2,1,0:T(8,128)(2,1)S(1)}, bf16[2,128,384]{...) custom-call(s32[3]{0:T(128)S(1)} %pad_add_fusion.place_ref, ...), custom_call_target="tpu_custom_call" | custom-call | tf_op jit(solution)/shard_map/pallas_call | solution.py:28
  2.9 0.6 collective-permute-start
  3.4 2.6 %collective-permute-start.1 = (bf16[2,128,384]{2,1,0:T(8,128)(2,1)S(1)}, bf16[2,128,384]{2,1,0:T(8,128)(2,1)S(1)}, u32[]{:S(2)}, u32[]{:S(2)}) collective-permute-start(bf16[2,128,384]{2,1,0:T(8,128)(2,1)S(1)} %get-tuple-element.43), channel_id=1, source_target_pairs={{0,2},{1,3},{2,0},{3,1},{4,6},{5,7},{6,4},{7,5},{8,10},{9,11},{10,... | collective-permute-start | bytes 589832 | tf_op jit(solution)/shard_map/ppermute | solution.py:450
  6.0 0.0 collective-permute-start.2
  6.0 5.7 %collective-permute-done.1.refs_0_.refs_2_.refs_5_ = bf16[2,128,384]{2,1,0:T(8,128)(2,1)S(1)} collective-permute-done((bf16[2,128,384]{2,1,0:T(8,128)(2,1)S(1)}, bf16[2,128,384]{2,1,0:T(8,128)(2,1)S(1)}, u32[]{:S(2)}, u32[]{:S(2)}) %collective-permute-start.1) | collective-permute-done | bytes 196640 | tf_op jit(solution)/shard_map/ppermute | solution.py:450
  11.8 3.7 %collective-permute-done.2.refs_1_.refs_3_.refs_6_ = bf16[2,128,384]{2,1,0:T(8,128)(2,1)S(1)} collective-permute-done((bf16[2,128,384]{2,1,0:T(8,128)(2,1)S(1)}, bf16[2,128,384]{2,1,0:T(8,128)(2,1)S(1)}, u32[]{:S(2)}, u32[]{:S(2)}) %collective-permute-start.2) | collective-permute-done | bytes 196640 | tf_op jit(solution)/shard_map/ppermute | solution.py:450
  15.5 0.0 copy-start
  15.5 3.5 %collective-permute-start.6 = (bf16[2,2,128,384]{3,2,1,0:T(8,128)(2,1)S(1)}, bf16[2,2,128,384]{3,2,1,0:T(8,128)(2,1)S(1)}, u32[]{:S(2)}, u32[]{:S(2)}) collective-permute-start(bf16[2,2,128,384]{3,2,1,0:T(8,128)(2,1)S(1)} %shard_map.156), channel_id=1, source_target_pairs={{0,4},{1,5},{4,8},{5,9},{6,2},{7,3},{8,12},{9,13},{10,6},{11,7},{1... | collective-permute-start | bytes 1179656 | tf_op jit(solution)/shard_map/ppermute | solution.py:450
  19.0 0.1 shard_map.155
  19.1 1.3 %collective-permute-start.5 = (bf16[2,2,128,384]{3,2,1,0:T(8,128)(2,1)S(1)}, bf16[2,2,128,384]{3,2,1,0:T(8,128)(2,1)S(1)}, u32[]{:S(2)}, u32[]{:S(2)}) collective-permute-start(bf16[2,2,128,384]{3,2,1,0:T(8,128)(2,1)S(1)} %get-tuple-element.47), channel_id=1, source_target_pairs={{2,6},{3,7},{4,0},{5,1},{6,10},{7,11},{8,4},{9,5},{10,14},{11,15},... | collective-permute-start | bytes 1179656 | tf_op jit(solution)/shard_map/ppermute | solution.py:450
  20.4 2.6 %collective-permute-start.3 = (bf16[2,128,384]{2,1,0:T(8,128)(2,1)S(1)}, bf16[2,128,384]{2,1,0:T(8,128)(2,1)S(1)}, u32[]{:S(2)}, u32[]{:S(2)}) collective-permute-start(bf16[2,128,384]{2,1,0:T(8,128)(2,1)S(1)} %get-tuple-element.45), channel_id=1, source_target_pairs={{0,2},{1,3},{2,0},{3,1},{4,6},{5,7},{6,4},{7,5},{8,10},{9,11},{10,... | collective-permute-start | bytes 589832 | tf_op jit(solution)/shard_map/ppermute | solution.py:450
  23.0 0.0 collective-permute-start.4
  23.6 1.8 %shard_map.157 = (bf16[2,256,384]{2,1,0:T(8,128)(2,1)S(1)}, f32[2,128]{1,0:T(2,128)S(1)}, f32[3,256,128]{2,1,0:T(8,128)S(1)}) custom-call(s32[3]{0:T(128)S(1)} %pad_add_fusion.place_ref, bf16[256,1536]{1,0:T(8,128)(2,1)} %bitcast.23, bf16[256,1536]{1,0:T(8,128)(2,1)} %bitcast.24, f32[1,128]{1,0:T(1,128)} %bitcast.33, f32[1,128]{1,0:T(1,128)} %bitcast.34, ...), custom_call_target="tpu_custom_call" | custom-call | tf_op jit(solution)/shard_map/pallas_call | solution.py:28
  25.5 3.3 %collective-permute-done.3.refs_4_.refs_0_ = bf16[2,128,384]{2,1,0:T(8,128)(2,1)S(1)} collective-permute-done((bf16[2,128,384]{2,1,0:T(8,128)(2,1)S(1)}, bf16[2,128,384]{2,1,0:T(8,128)(2,1)S(1)}, u32[]{:S(2)}, u32[]{:S(2)}) %collective-permute-start.3) | collective-permute-done | bytes 196640 | tf_op jit(solution)/shard_map/ppermute | solution.py:450
  28.7 2.6 %collective-permute-done.4.refs_5_.refs_1_ = bf16[2,128,384]{2,1,0:T(8,128)(2,1)S(1)} collective-permute-done((bf16[2,128,384]{2,1,0:T(8,128)(2,1)S(1)}, bf16[2,128,384]{2,1,0:T(8,128)(2,1)S(1)}, u32[]{:S(2)}, u32[]{:S(2)}) %collective-permute-start.4) | collective-permute-done | bytes 196640 | tf_op jit(solution)/shard_map/ppermute | solution.py:450
  31.3 0.7 collective-permute-done.5.refs_6_
  32.1 8.8 %shard_map.158 = (bf16[1,128,384]{2,1,0:T(8,128)(2,1)S(1)}, bf16[1,128,384]{2,1,0:T(8,128)(2,1)S(1)}, bf16[1,128,384]{2,1,0:T(8,128)(2,1)S(1)}, bf16[1,128,384]{...) custom-call(s32[3]{0:T(128)S(1)} %pad_add_fusion.place_ref, ...), custom_call_target="tpu_custom_call" | custom-call | tf_op jit(solution)/shard_map/pallas_call | solution.py:28
  40.9 1.6 %collective-permute-start.17 = (f32[128,384]{1,0:T(8,128)S(1)}, f32[128,384]{1,0:T(8,128)S(1)}, u32[]{:S(2)}, u32[]{:S(2)}) collective-permute-start(f32[128,384]{1,0:T(8,128)S(1)} %get-tuple-element.66), channel_id=1, source_target_pairs={{0,4},{1,5},{2,6},{3,7},{4,8},{5,9},{6,10},{7,11},{8,12},{9,13},{1... | collective-permute-start | bytes 589832 | tf_op jit(solution)/shard_map/ppermute | solution.py:450
  42.5 1.7 %collective-permute-start.18 = (f32[128,384]{1,0:T(8,128)S(1)}, f32[128,384]{1,0:T(8,128)S(1)}, u32[]{:S(2)}, u32[]{:S(2)}) collective-permute-start(f32[128,384]{1,0:T(8,128)S(1)} %get-tuple-element.67), channel_id=1, source_target_pairs={{0,8},{1,9},{2,10},{3,11},{4,12},{5,13},{6,14},{7,15},{8,0},{9,1},... | collective-permute-start | bytes 589832 | tf_op jit(solution)/shard_map/ppermute | solution.py:450
  44.2 2.2 %collective-permute-start.19 = (f32[128,384]{1,0:T(8,128)S(1)}, f32[128,384]{1,0:T(8,128)S(1)}, u32[]{:S(2)}, u32[]{:S(2)}) collective-permute-start(f32[128,384]{1,0:T(8,128)S(1)} %get-tuple-element.68), channel_id=1, source_target_pairs={{0,12},{1,13},{2,14},{3,15},{4,0},{5,1},{6,2},{7,3},{8,4},{9,5},{1... | collective-permute-start | bytes 589832 | tf_op jit(solution)/shard_map/ppermute | solution.py:450
  46.4 1.5 %collective-permute-start.20 = (f32[2,128]{1,0:T(2,128)S(1)}, f32[2,128]{1,0:T(2,128)S(1)}, u32[]{:S(2)}, u32[]{:S(2)}) collective-permute-start(f32[2,128]{1,0:T(2,128)S(1)} %get-tuple-element.69.refs_4_), channel_id=1, source_target_pairs={{0,16},{16,0},{1,17},{17,1},{2,18},{18,2},{3,19},{19,3},{4,20},{20... | collective-permute-start | bytes 3080 | tf_op jit(solution)/shard_map/ppermute | solution.py:450
  47.9 2.0 %collective-permute-done.20.refs_5_ = f32[2,128]{1,0:T(2,128)S(1)} collective-permute-done((f32[2,128]{1,0:T(2,128)S(1)}, f32[2,128]{1,0:T(2,128)S(1)}, u32[]{:S(2)}, u32[]{:S(2)}) %collective-permute-start.20) | collective-permute-done | bytes 1056 | tf_op jit(solution)/shard_map/ppermute | solution.py:450
  50.0 0.6 collective-permute-done.17.refs_1_
  50.6 7.6 %collective-permute-done.18.refs_2_ = f32[128,384]{1,0:T(8,128)S(1)} collective-permute-done((f32[128,384]{1,0:T(8,128)S(1)}, f32[128,384]{1,0:T(8,128)S(1)}, u32[]{:S(2)}, u32[]{:S(2)}) %collective-permute-start.18) | collective-permute-done | bytes 196640 | tf_op jit(solution)/shard_map/ppermute | solution.py:450
  58.2 0.0 collective-permute-done.19.refs_3_
  58.3 5.8 %collective-permute-start.25 = (bf16[136,384]{1,0:T(8,128)(2,1)S(1)}, bf16[136,384]{1,0:T(8,128)(2,1)S(1)}, u32[]{:S(2)}, u32[]{:S(2)}) collective-permute-start(bf16[136,384]{1,0:T(8,128)(2,1)S(1)} %shard_map.163.refs_0_), channel_id=1, source_target_pairs={{0,12},{1,13},{2,14},{3,15},{4,0},{5,1},{6,2},{7,3},{8,4},{9,5},{1... | collective-permute-start | bytes 313352 | tf_op jit(solution)/shard_map/ppermute | solution.py:450
  64.1 0.4 collective-permute-start.24
  64.5 0.2 collective-permute-start.23
  64.8 4.8 %collective-permute-start.13 = (bf16[2,2,128,384]{3,2,1,0:T(8,128)(2,1)S(1)}, bf16[2,2,128,384]{3,2,1,0:T(8,128)(2,1)S(1)}, u32[]{:S(2)}, u32[]{:S(2)}) collective-permute-start(bf16[2,2,128,384]{3,2,1,0:T(8,128)(2,1)S(1)} %shard_map.160), channel_id=1, source_target_pairs={{0,4},{1,5},{4,8},{5,9},{6,2},{7,3},{8,12},{9,13},{10,6},{11,7},{1... | collective-permute-start | bytes 1179656 | tf_op jit(solution)/shard_map/ppermute | solution.py:450
  69.5 1.3 %collective-permute-start.12 = (bf16[2,2,128,384]{3,2,1,0:T(8,128)(2,1)S(1)}, bf16[2,2,128,384]{3,2,1,0:T(8,128)(2,1)S(1)}, u32[]{:S(2)}, u32[]{:S(2)}) collective-permute-start(bf16[2,2,128,384]{3,2,1,0:T(8,128)(2,1)S(1)} %get-tuple-element.58), channel_id=1, source_target_pairs={{2,6},{3,7},{4,0},{5,1},{6,10},{7,11},{8,4},{9,5},{10,14},{11,15},... | collective-permute-start | bytes 1179656 | tf_op jit(solution)/shard_map/ppermute | solution.py:450
  70.8 0.0 collective-permute-done.25
  70.9 4.1 %collective-permute-done.24 = bf16[136,384]{1,0:T(8,128)(2,1)S(1)} collective-permute-done((bf16[136,384]{1,0:T(8,128)(2,1)S(1)}, bf16[136,384]{1,0:T(8,128)(2,1)S(1)}, u32[]{:S(2)}, u32[]{:S(2)}) %collective-permute-start.24) | collective-permute-done | bytes 104480 | tf_op jit(solution)/shard_map/ppermute | solution.py:450
  75.0 0.1 pad_maximum_fusion.refs_2_
  75.0 1.0 collective-permute-start.26
  76.0 2.2 %collective-permute-start.10 = (f32[8,384]{1,0:T(8,128)S(1)}, f32[8,384]{1,0:T(8,128)S(1)}, u32[]{:S(2)}, u32[]{:S(2)}) collective-permute-start(f32[8,384]{1,0:T(8,128)S(1)} %get-tuple-element.56), channel_id=1, source_target_pairs={{0,4},{1,5},{2,6},{3,7},{4,8},{5,9},{6,10},{7,11},{8,12},{9,13},{1... | collective-permute-start | bytes 36872 | tf_op jit(solution)/shard_map/ppermute | solution.py:450
  78.2 1.3 %collective-permute-start.11 = (f32[8,384]{1,0:T(8,128)S(1)}, f32[8,384]{1,0:T(8,128)S(1)}, u32[]{:S(2)}, u32[]{:S(2)}) collective-permute-start(f32[8,384]{1,0:T(8,128)S(1)} %get-tuple-element.57), channel_id=1, source_target_pairs={{4,0},{5,1},{6,2},{7,3},{8,4},{9,5},{10,6},{11,7},{12,8},{13,9},{1... | collective-permute-start | bytes 36872 | tf_op jit(solution)/shard_map/ppermute | solution.py:450
  79.5 0.1 collective-permute-start.7
  79.6 2.7 %collective-permute-done.12.refs_7_ = bf16[2,2,128,384]{3,2,1,0:T(8,128)(2,1)S(1)} collective-permute-done((bf16[2,2,128,384]{3,2,1,0:T(8,128)(2,1)S(1)}, bf16[2,2,128,384]{3,2,1,0:T(8,128)(2,1)S(1)}, u32[]{:S(2)}, u32[]{:S(2)}) %collective-permute-start.12) | collective-permute-done | bytes 393248 | tf_op jit(solution)/shard_map/ppermute | solution.py:450
  82.3 1.3 %collective-permute-start.8 = (bf16[1,128,384]{2,1,0:T(8,128)(2,1)S(1)}, bf16[1,128,384]{2,1,0:T(8,128)(2,1)S(1)}, u32[]{:S(2)}, u32[]{:S(2)}) collective-permute-start(bf16[1,128,384]{2,1,0:T(8,128)(2,1)S(1)} %get-tuple-element.53), channel_id=1, source_target_pairs={{0,2},{1,3},{2,0},{3,1},{4,6},{5,7},{6,4},{7,5},{8,10},{9,11},{10,... | collective-permute-start | bytes 294920 | tf_op jit(solution)/shard_map/ppermute | solution.py:450
  83.6 0.0 collective-permute-done.10.refs_1_
  83.6 0.6 collective-permute-done.11.refs_2_
  84.2 3.5 %shard_map.161 = (bf16[2,128,384]{2,1,0:T(8,128)(2,1)S(1)}, bf16[2,128,384]{2,1,0:T(8,128)(2,1)S(1)}, bf16[2,128,384]{2,1,0:T(8,128)(2,1)S(1)}, bf16[2,128,384]{2,1,0:T(8,128)(2,1)S(1)}) custom-call(s32[3]{0:T(128)S(1)} %pad_add_fusion.place_ref, s32[3,12]{1,0:T(4,128)S(1)} %bitcast.20, f32[2,512,384]{2,1,0:T(8,128)S(1)} %get-tuple-element.55.refs_0_, ...), custom_call_target="tpu_custom_call" | custom-call | tf_op jit(solution)/shard_map/pallas_call | solution.py:28
  87.8 0.1 collective-permute-start.14
  87.8 0.5 collective-permute-start.29
  88.3 0.0 collective-permute-done.26.refs_2_
  88.3 0.1 collective-permute-start.27
  88.4 0.1 collective-permute-start.9
  88.6 0.0 collective-permute-done.8.refs_2_
  88.6 1.9 %collective-permute-start.15 = (bf16[2,128,384]{2,1,0:T(8,128)(2,1)S(1)}, bf16[2,128,384]{2,1,0:T(8,128)(2,1)S(1)}, u32[]{:S(2)}, u32[]{:S(2)}) collective-permute-start(bf16[2,128,384]{2,1,0:T(8,128)(2,1)S(1)} %get-tuple-element.61), channel_id=1, source_target_pairs={{0,2},{1,3},{2,0},{3,1},{4,6},{5,7},{6,4},{7,5},{8,10},{9,11},{10,... | collective-permute-start | bytes 589832 | tf_op jit(solution)/shard_map/ppermute | solution.py:450
  90.5 2.4 %collective-permute-done.9.refs_3_ = bf16[1,128,384]{2,1,0:T(8,128)(2,1)S(1)} collective-permute-done((bf16[1,128,384]{2,1,0:T(8,128)(2,1)S(1)}, bf16[1,128,384]{2,1,0:T(8,128)(2,1)S(1)}, u32[]{:S(2)}, u32[]{:S(2)}) %collective-permute-start.9) | collective-permute-done | bytes 98336 | tf_op jit(solution)/shard_map/ppermute | solution.py:450
  92.9 0.8 collective-permute-start.21
  93.7 0.0 collective-permute-done.14.refs_1_
  93.7 1.6 %collective-permute-start.16 = (bf16[2,128,384]{2,1,0:T(8,128)(2,1)S(1)}, bf16[2,128,384]{2,1,0:T(8,128)(2,1)S(1)}, u32[]{:S(2)}, u32[]{:S(2)}) collective-permute-start(bf16[2,128,384]{2,1,0:T(8,128)(2,1)S(1)} %get-tuple-element.62), channel_id=1, source_target_pairs={{0,3},{1,2},{2,1},{3,0},{4,7},{5,6},{6,5},{7,4},{8,11},{9,10},{10,... | collective-permute-start | bytes 589832 | tf_op jit(solution)/shard_map/ppermute | solution.py:450
  95.3 3.0 %collective-permute-done.15.refs_2_ = bf16[2,128,384]{2,1,0:T(8,128)(2,1)S(1)} collective-permute-done((bf16[2,128,384]{2,1,0:T(8,128)(2,1)S(1)}, bf16[2,128,384]{2,1,0:T(8,128)(2,1)S(1)}, u32[]{:S(2)}, u32[]{:S(2)}) %collective-permute-start.15) | collective-permute-done | bytes 196640 | tf_op jit(solution)/shard_map/ppermute | solution.py:450
  98.4 2.2 %collective-permute-done.21.refs_0_ = bf16[136,384]{1,0:T(8,128)(2,1)S(1)} collective-permute-done((bf16[136,384]{1,0:T(8,128)(2,1)S(1)}, bf16[136,384]{1,0:T(8,128)(2,1)S(1)}, u32[]{:S(2)}, u32[]{:S(2)}) %collective-permute-start.21) | collective-permute-done | bytes 104480 | tf_op jit(solution)/shard_map/ppermute | solution.py:450
  100.6 1.3 %shard_map.159 = bf16[128,1536]{1,0:T(8,128)(2,1)} custom-call(s32[3]{0:T(128)S(1)} %pad_add_fusion.place_ref, bf16[1,128,384]{2,1,0:T(8,128)(2,1)S(1)} %get-tuple-element.51.refs_0_, bf16[1,128,384]{2,1,0:T(8,128)(2,1)S(1)} %collective-permute-done.7.refs_1_, bf16[1,128,384]{2,1,0:T(8,128)(2,1)S(1)} %collective-permute-done.8.refs_2_, ...), custom_call_target="tpu_custom_call" | custom-call | tf_op jit(solution)/shard_map/pallas_call | solution.py:28
  101.9 1.7 %collective-permute-done.16.refs_3_ = bf16[2,128,384]{2,1,0:T(8,128)(2,1)S(1)} collective-permute-done((bf16[2,128,384]{2,1,0:T(8,128)(2,1)S(1)}, bf16[2,128,384]{2,1,0:T(8,128)(2,1)S(1)}, u32[]{:S(2)}, u32[]{:S(2)}) %collective-permute-start.16) | collective-permute-done | bytes 196640 | tf_op jit(solution)/shard_map/ppermute | solution.py:450
  103.6 1.5 %shard_map.162 = (bf16[128,1536]{1,0:T(8,128)(2,1)}, bf16[128,1536]{1,0:T(8,128)(2,1)}) custom-call(s32[3]{0:T(128)S(1)} %pad_add_fusion.place_ref, bf16[2,128,384]{2,1,0:T(8,128)(2,1)S(1)} %get-tuple-element.59.refs_0_, bf16[2,128,384]{2,1,0:T(8,128)(2,1)S(1)} %collective-permute-done.14.refs_1_, bf16[2,128,384]{2,1,0:T(8,128)(2,1)S(1)} %collective-permute-done.15.refs_2_, ...), custom_call_target="tpu_custom_call" | custom-call | tf_op jit(solution)/shard_map/pallas_call | solution.py:28
  105.1 0.0 collective-permute-done.28.refs_1_
  105.1 1.8 %shard_map.164 = (f32[256,1536]{1,0:T(8,128)}, f32[256,1536]{1,0:T(8,128)}, f32[2,128]{1,0:T(2,128)S(1)}) custom-call(s32[3]{0:T(128)S(1)} %pad_add_fusion.place_ref, bf16[136,384]{1,0:T(8,128)(2,1)S(1)} %shard_map.163.refs_0_, bf16[136,384]{1,0:T(8,128)(2,1)S(1)} %collective-permute-done.28.refs_1_, bf16[3,136,384]{2,1,0:T(8,128)(2,1)S(1)} %pad_maximum_fusion.refs_2_, ...), custom_call_target="tpu_custom_call" | custom-call | tf_op jit(solution)/shard_map/pallas_call | solution.py:28
  106.9 0.0 collective-permute-done.22.refs_1_
  106.9 0.0 collective-permute-done.27.refs_3_
  106.9 2.3 %shard_map.165 = (f32[256,1536]{1,0:T(8,128)}, f32[256,1536]{1,0:T(8,128)}, f32[2,128]{1,0:T(2,128)}) custom-call(s32[3]{0:T(128)S(1)} %pad_add_fusion.place_ref, bf16[136,384]{1,0:T(8,128)(2,1)S(1)} %collective-permute-done.21.refs_0_, bf16[136,384]{1,0:T(8,128)(2,1)S(1)} %collective-permute-done.22.refs_1_, ...), custom_call_target="tpu_custom_call", output_to_operand_aliasing={{0}: (6, {}), {1}: (7, {})} | custom-call | tf_op jit(solution)/shard_map/pallas_call | solution.py:28
  (12 shorter events, 0.1 us)
Async XLA Ops:
  2.9 16.1 %collective-permute-start = (bf16[4,128,384]{2,1,0:T(8,128)(2,1)S(1)}, bf16[4,128,384]{2,1,0:T(8,128)(2,1)S(1)}, u32[]{:S(2)}, u32[]{:S(2)}) collective-permute-start(bf16[4,128,384]{2,1,0:T(8,128)(2,1)S(1)} %get-tuple-element.42), channel_id=1, source_target_pairs={{0,1},{1,0},{2,3},{3,2},{4,5},{5,4},{6,7},{7,6},{8,9},{9,8},{10,11... | collective-permute-start | bytes 1179656 | tf_op jit(solution)/shard_map/ppermute | solution.py:450
  3.4 8.3 %collective-permute-start.1 = (bf16[2,128,384]{2,1,0:T(8,128)(2,1)S(1)}, bf16[2,128,384]{2,1,0:T(8,128)(2,1)S(1)}, u32[]{:S(2)}, u32[]{:S(2)}) collective-permute-start(bf16[2,128,384]{2,1,0:T(8,128)(2,1)S(1)} %get-tuple-element.43), channel_id=1, source_target_pairs={{0,2},{1,3},{2,0},{3,1},{4,6},{5,7},{6,4},{7,5},{8,10},{9,11},{10,... | collective-permute-start | bytes 589832 | tf_op jit(solution)/shard_map/ppermute | solution.py:450
  6.0 9.4 %collective-permute-start.2 = (bf16[2,128,384]{2,1,0:T(8,128)(2,1)S(1)}, bf16[2,128,384]{2,1,0:T(8,128)(2,1)S(1)}, u32[]{:S(2)}, u32[]{:S(2)}) collective-permute-start(bf16[2,128,384]{2,1,0:T(8,128)(2,1)S(1)} %get-tuple-element.44), channel_id=1, source_target_pairs={{0,3},{1,2},{2,1},{3,0},{4,7},{5,6},{6,5},{7,4},{8,11},{9,10},{10,... | collective-permute-start | bytes 589832 | tf_op jit(solution)/shard_map/ppermute | solution.py:450
  15.5 16.6 %copy-start = (s32[12,3]{0,1:T(4,128)S(1)}, s32[12,3]{0,1:T(4,128)}, u32[]{:S(2)}) copy-start(s32[12,3]{0,1:T(4,128)} %param.18) | copy-start | bytes 436
  15.5 15.8 %collective-permute-start.6 = (bf16[2,2,128,384]{3,2,1,0:T(8,128)(2,1)S(1)}, bf16[2,2,128,384]{3,2,1,0:T(8,128)(2,1)S(1)}, u32[]{:S(2)}, u32[]{:S(2)}) collective-permute-start(bf16[2,2,128,384]{3,2,1,0:T(8,128)(2,1)S(1)} %shard_map.156), channel_id=1, source_target_pairs={{0,4},{1,5},{4,8},{5,9},{6,2},{7,3},{8,12},{9,13},{10,6},{11,7},{1... | collective-permute-start | bytes 1179656 | tf_op jit(solution)/shard_map/ppermute | solution.py:450
  19.1 13.0 %collective-permute-start.5 = (bf16[2,2,128,384]{3,2,1,0:T(8,128)(2,1)S(1)}, bf16[2,2,128,384]{3,2,1,0:T(8,128)(2,1)S(1)}, u32[]{:S(2)}, u32[]{:S(2)}) collective-permute-start(bf16[2,2,128,384]{3,2,1,0:T(8,128)(2,1)S(1)} %get-tuple-element.47), channel_id=1, source_target_pairs={{2,6},{3,7},{4,0},{5,1},{6,10},{7,11},{8,4},{9,5},{10,14},{11,15},... | collective-permute-start | bytes 1179656 | tf_op jit(solution)/shard_map/ppermute | solution.py:450
  20.4 8.4 %collective-permute-start.3 = (bf16[2,128,384]{2,1,0:T(8,128)(2,1)S(1)}, bf16[2,128,384]{2,1,0:T(8,128)(2,1)S(1)}, u32[]{:S(2)}, u32[]{:S(2)}) collective-permute-start(bf16[2,128,384]{2,1,0:T(8,128)(2,1)S(1)} %get-tuple-element.45), channel_id=1, source_target_pairs={{0,2},{1,3},{2,0},{3,1},{4,6},{5,7},{6,4},{7,5},{8,10},{9,11},{10,... | collective-permute-start | bytes 589832 | tf_op jit(solution)/shard_map/ppermute | solution.py:450
  23.0 8.3 %collective-permute-start.4 = (bf16[2,128,384]{2,1,0:T(8,128)(2,1)S(1)}, bf16[2,128,384]{2,1,0:T(8,128)(2,1)S(1)}, u32[]{:S(2)}, u32[]{:S(2)}) collective-permute-start(bf16[2,128,384]{2,1,0:T(8,128)(2,1)S(1)} %get-tuple-element.46), channel_id=1, source_target_pairs={{0,3},{1,2},{2,1},{3,0},{4,7},{5,6},{6,5},{7,4},{8,11},{9,10},{10,... | collective-permute-start | bytes 589832 | tf_op jit(solution)/shard_map/ppermute | solution.py:450
  40.9 9.8 %collective-permute-start.17 = (f32[128,384]{1,0:T(8,128)S(1)}, f32[128,384]{1,0:T(8,128)S(1)}, u32[]{:S(2)}, u32[]{:S(2)}) collective-permute-start(f32[128,384]{1,0:T(8,128)S(1)} %get-tuple-element.66), channel_id=1, source_target_pairs={{0,4},{1,5},{2,6},{3,7},{4,8},{5,9},{6,10},{7,11},{8,12},{9,13},{1... | collective-permute-start | bytes 589832 | tf_op jit(solution)/shard_map/ppermute | solution.py:450
  42.5 15.8 %collective-permute-start.18 = (f32[128,384]{1,0:T(8,128)S(1)}, f32[128,384]{1,0:T(8,128)S(1)}, u32[]{:S(2)}, u32[]{:S(2)}) collective-permute-start(f32[128,384]{1,0:T(8,128)S(1)} %get-tuple-element.67), channel_id=1, source_target_pairs={{0,8},{1,9},{2,10},{3,11},{4,12},{5,13},{6,14},{7,15},{8,0},{9,1},... | collective-permute-start | bytes 589832 | tf_op jit(solution)/shard_map/ppermute | solution.py:450
  44.2 14.0 %collective-permute-start.19 = (f32[128,384]{1,0:T(8,128)S(1)}, f32[128,384]{1,0:T(8,128)S(1)}, u32[]{:S(2)}, u32[]{:S(2)}) collective-permute-start(f32[128,384]{1,0:T(8,128)S(1)} %get-tuple-element.68), channel_id=1, source_target_pairs={{0,12},{1,13},{2,14},{3,15},{4,0},{5,1},{6,2},{7,3},{8,4},{9,5},{1... | collective-permute-start | bytes 589832 | tf_op jit(solution)/shard_map/ppermute | solution.py:450
  46.4 3.6 %collective-permute-start.20 = (f32[2,128]{1,0:T(2,128)S(1)}, f32[2,128]{1,0:T(2,128)S(1)}, u32[]{:S(2)}, u32[]{:S(2)}) collective-permute-start(f32[2,128]{1,0:T(2,128)S(1)} %get-tuple-element.69.refs_4_), channel_id=1, source_target_pairs={{0,16},{16,0},{1,17},{17,1},{2,18},{18,2},{3,19},{19,3},{4,20},{20... | collective-permute-start | bytes 3080 | tf_op jit(solution)/shard_map/ppermute | solution.py:450
  58.3 12.5 %collective-permute-start.25 = (bf16[136,384]{1,0:T(8,128)(2,1)S(1)}, bf16[136,384]{1,0:T(8,128)(2,1)S(1)}, u32[]{:S(2)}, u32[]{:S(2)}) collective-permute-start(bf16[136,384]{1,0:T(8,128)(2,1)S(1)} %shard_map.163.refs_0_), channel_id=1, source_target_pairs={{0,12},{1,13},{2,14},{3,15},{4,0},{5,1},{6,2},{7,3},{8,4},{9,5},{1... | collective-permute-start | bytes 313352 | tf_op jit(solution)/shard_map/ppermute | solution.py:450
  64.1 10.9 %collective-permute-start.24 = (bf16[136,384]{1,0:T(8,128)(2,1)S(1)}, bf16[136,384]{1,0:T(8,128)(2,1)S(1)}, u32[]{:S(2)}, u32[]{:S(2)}) collective-permute-start(bf16[136,384]{1,0:T(8,128)(2,1)S(1)} %shard_map.163.refs_0_), channel_id=1, source_target_pairs={{0,8},{1,9},{2,10},{3,11},{4,12},{5,13},{6,14},{7,15},{8,0},{9,1},... | collective-permute-start | bytes 313352 | tf_op jit(solution)/shard_map/ppermute | solution.py:450
  64.5 10.5 %collective-permute-start.23 = (bf16[136,384]{1,0:T(8,128)(2,1)S(1)}, bf16[136,384]{1,0:T(8,128)(2,1)S(1)}, u32[]{:S(2)}, u32[]{:S(2)}) collective-permute-start(bf16[136,384]{1,0:T(8,128)(2,1)S(1)} %shard_map.163.refs_0_), channel_id=1, source_target_pairs={{0,4},{1,5},{2,6},{3,7},{4,8},{5,9},{6,10},{7,11},{8,12},{9,13},{1... | collective-permute-start | bytes 313352 | tf_op jit(solution)/shard_map/ppermute | solution.py:450
  64.8 14.7 %collective-permute-start.13 = (bf16[2,2,128,384]{3,2,1,0:T(8,128)(2,1)S(1)}, bf16[2,2,128,384]{3,2,1,0:T(8,128)(2,1)S(1)}, u32[]{:S(2)}, u32[]{:S(2)}) collective-permute-start(bf16[2,2,128,384]{3,2,1,0:T(8,128)(2,1)S(1)} %shard_map.160), channel_id=1, source_target_pairs={{0,4},{1,5},{4,8},{5,9},{6,2},{7,3},{8,12},{9,13},{10,6},{11,7},{1... | collective-permute-start | bytes 1179656 | tf_op jit(solution)/shard_map/ppermute | solution.py:450
  69.5 12.8 %collective-permute-start.12 = (bf16[2,2,128,384]{3,2,1,0:T(8,128)(2,1)S(1)}, bf16[2,2,128,384]{3,2,1,0:T(8,128)(2,1)S(1)}, u32[]{:S(2)}, u32[]{:S(2)}) collective-permute-start(bf16[2,2,128,384]{3,2,1,0:T(8,128)(2,1)S(1)} %get-tuple-element.58), channel_id=1, source_target_pairs={{2,6},{3,7},{4,0},{5,1},{6,10},{7,11},{8,4},{9,5},{10,14},{11,15},... | collective-permute-start | bytes 1179656 | tf_op jit(solution)/shard_map/ppermute | solution.py:450
  75.0 13.3 %collective-permute-start.26 = (bf16[3,136,384]{2,1,0:T(8,128)(2,1)S(1)}, bf16[3,136,384]{2,1,0:T(8,128)(2,1)S(1)}, u32[]{:S(2)}, u32[]{:S(2)}) collective-permute-start(bf16[3,136,384]{2,1,0:T(8,128)(2,1)S(1)} %pad_maximum_fusion.refs_2_), channel_id=1, source_target_pairs={{0,2},{1,3},{2,0},{3,1},{4,6},{5,7},{6,4},{7,5},{8,10},{9,11},{10,... | collective-permute-start | bytes 940040 | tf_op jit(solution)/shard_map/ppermute | solution.py:450
  76.0 7.6 %collective-permute-start.10 = (f32[8,384]{1,0:T(8,128)S(1)}, f32[8,384]{1,0:T(8,128)S(1)}, u32[]{:S(2)}, u32[]{:S(2)}) collective-permute-start(f32[8,384]{1,0:T(8,128)S(1)} %get-tuple-element.56), channel_id=1, source_target_pairs={{0,4},{1,5},{2,6},{3,7},{4,8},{5,9},{6,10},{7,11},{8,12},{9,13},{1... | collective-permute-start | bytes 36872 | tf_op jit(solution)/shard_map/ppermute | solution.py:450
  78.2 6.1 %collective-permute-start.11 = (f32[8,384]{1,0:T(8,128)S(1)}, f32[8,384]{1,0:T(8,128)S(1)}, u32[]{:S(2)}, u32[]{:S(2)}) collective-permute-start(f32[8,384]{1,0:T(8,128)S(1)} %get-tuple-element.57), channel_id=1, source_target_pairs={{4,0},{5,1},{6,2},{7,3},{8,4},{9,5},{10,6},{11,7},{12,8},{13,9},{1... | collective-permute-start | bytes 36872 | tf_op jit(solution)/shard_map/ppermute | solution.py:450
  79.5 8.9 %collective-permute-start.7 = (bf16[1,128,384]{2,1,0:T(8,128)(2,1)S(1)}, bf16[1,128,384]{2,1,0:T(8,128)(2,1)S(1)}, u32[]{:S(2)}, u32[]{:S(2)}) collective-permute-start(bf16[1,128,384]{2,1,0:T(8,128)(2,1)S(1)} %get-tuple-element.52), channel_id=1, source_target_pairs={{0,1},{1,0},{2,3},{3,2},{4,5},{5,4},{6,7},{7,6},{8,9},{9,8},{10,11... | collective-permute-start | bytes 294920 | tf_op jit(solution)/shard_map/ppermute | solution.py:450
  82.3 6.3 %collective-permute-start.8 = (bf16[1,128,384]{2,1,0:T(8,128)(2,1)S(1)}, bf16[1,128,384]{2,1,0:T(8,128)(2,1)S(1)}, u32[]{:S(2)}, u32[]{:S(2)}) collective-permute-start(bf16[1,128,384]{2,1,0:T(8,128)(2,1)S(1)} %get-tuple-element.53), channel_id=1, source_target_pairs={{0,2},{1,3},{2,0},{3,1},{4,6},{5,7},{6,4},{7,5},{8,10},{9,11},{10,... | collective-permute-start | bytes 294920 | tf_op jit(solution)/shard_map/ppermute | solution.py:450
  87.8 5.9 %collective-permute-start.14 = (bf16[2,128,384]{2,1,0:T(8,128)(2,1)S(1)}, bf16[2,128,384]{2,1,0:T(8,128)(2,1)S(1)}, u32[]{:S(2)}, u32[]{:S(2)}) collective-permute-start(bf16[2,128,384]{2,1,0:T(8,128)(2,1)S(1)} %get-tuple-element.60), channel_id=1, source_target_pairs={{0,1},{1,0},{2,3},{3,2},{4,5},{5,4},{6,7},{7,6},{8,9},{9,8},{10,11... | collective-permute-start | bytes 589832 | tf_op jit(solution)/shard_map/ppermute | solution.py:450
  87.8 17.2 %collective-permute-start.29 = (bf16[3,136,384]{2,1,0:T(8,128)(2,1)S(1)}, bf16[3,136,384]{2,1,0:T(8,128)(2,1)S(1)}, u32[]{:S(2)}, u32[]{:S(2)}) collective-permute-start(bf16[3,136,384]{2,1,0:T(8,128)(2,1)S(1)} %pad_maximum_fusion.refs_2_), channel_id=1, source_target_pairs={{0,1},{1,0},{2,3},{3,2},{4,5},{5,4},{6,7},{7,6},{8,9},{9,8},{10,11... | collective-permute-start | bytes 940040 | tf_op jit(solution)/shard_map/ppermute | solution.py:450
  88.3 18.5 %collective-permute-start.27 = (bf16[3,136,384]{2,1,0:T(8,128)(2,1)S(1)}, bf16[3,136,384]{2,1,0:T(8,128)(2,1)S(1)}, u32[]{:S(2)}, u32[]{:S(2)}) collective-permute-start(bf16[3,136,384]{2,1,0:T(8,128)(2,1)S(1)} %collective-permute-done.26.refs_2_), channel_id=1, source_target_pairs={{0,1},{1,0},{2,3},{3,2},{4,5},{5,4},{6,7},{7,6},{8,9},{9,8},{10,11... | collective-permute-start | bytes 940040 | tf_op jit(solution)/shard_map/ppermute | solution.py:450
  88.4 4.5 %collective-permute-start.9 = (bf16[1,128,384]{2,1,0:T(8,128)(2,1)S(1)}, bf16[1,128,384]{2,1,0:T(8,128)(2,1)S(1)}, u32[]{:S(2)}, u32[]{:S(2)}) collective-permute-start(bf16[1,128,384]{2,1,0:T(8,128)(2,1)S(1)} %get-tuple-element.54), channel_id=1, source_target_pairs={{0,3},{1,2},{2,1},{3,0},{4,7},{5,6},{6,5},{7,4},{8,11},{9,10},{10,... | collective-permute-start | bytes 294920 | tf_op jit(solution)/shard_map/ppermute | solution.py:450
  88.6 9.8 %collective-permute-start.15 = (bf16[2,128,384]{2,1,0:T(8,128)(2,1)S(1)}, bf16[2,128,384]{2,1,0:T(8,128)(2,1)S(1)}, u32[]{:S(2)}, u32[]{:S(2)}) collective-permute-start(bf16[2,128,384]{2,1,0:T(8,128)(2,1)S(1)} %get-tuple-element.61), channel_id=1, source_target_pairs={{0,2},{1,3},{2,0},{3,1},{4,6},{5,7},{6,4},{7,5},{8,10},{9,11},{10,... | collective-permute-start | bytes 589832 | tf_op jit(solution)/shard_map/ppermute | solution.py:450
  92.9 7.7 %collective-permute-start.21 = (bf16[136,384]{1,0:T(8,128)(2,1)S(1)}, bf16[136,384]{1,0:T(8,128)(2,1)S(1)}, u32[]{:S(2)}, u32[]{:S(2)}) collective-permute-start(bf16[136,384]{1,0:T(8,128)(2,1)S(1)} %shard_map.163.refs_0_), channel_id=1, source_target_pairs={{0,2},{1,3},{2,0},{3,1},{4,6},{5,7},{6,4},{7,5},{8,10},{9,11},{10,... | collective-permute-start | bytes 313352 | tf_op jit(solution)/shard_map/ppermute | solution.py:450
  93.7 9.9 %collective-permute-start.16 = (bf16[2,128,384]{2,1,0:T(8,128)(2,1)S(1)}, bf16[2,128,384]{2,1,0:T(8,128)(2,1)S(1)}, u32[]{:S(2)}, u32[]{:S(2)}) collective-permute-start(bf16[2,128,384]{2,1,0:T(8,128)(2,1)S(1)} %get-tuple-element.62), channel_id=1, source_target_pairs={{0,3},{1,2},{2,1},{3,0},{4,7},{5,6},{6,5},{7,4},{8,11},{9,10},{10,... | collective-permute-start | bytes 589832 | tf_op jit(solution)/shard_map/ppermute | solution.py:450
  98.3 6.7 %collective-permute-start.28 = (bf16[136,384]{1,0:T(8,128)(2,1)S(1)}, bf16[136,384]{1,0:T(8,128)(2,1)S(1)}, u32[]{:S(2)}, u32[]{:S(2)}) collective-permute-start(bf16[136,384]{1,0:T(8,128)(2,1)S(1)} %shard_map.163.refs_0_), channel_id=1, source_target_pairs={{0,1},{1,0},{2,3},{3,2},{4,5},{5,4},{6,7},{7,6},{8,9},{9,8},{10,11... | collective-permute-start | bytes 313352 | tf_op jit(solution)/shard_map/ppermute | solution.py:450
  100.6 6.3 %collective-permute-start.22 = (bf16[136,384]{1,0:T(8,128)(2,1)S(1)}, bf16[136,384]{1,0:T(8,128)(2,1)S(1)}, u32[]{:S(2)}, u32[]{:S(2)}) collective-permute-start(bf16[136,384]{1,0:T(8,128)(2,1)S(1)} %collective-permute-done.21.refs_0_), channel_id=1, source_target_pairs={{0,1},{1,0},{2,3},{3,2},{4,5},{5,4},{6,7},{7,6},{8,9},{9,8},{10,11... | collective-permute-start | bytes 313352 | tf_op jit(solution)/shard_map/ppermute | solution.py:450
